TPU v7x, 32 devices: a whole 2x2x4 slice. The times are simulated.
32 devices in a mesh: dp: 8 (over z, y), tensor: 4 (over x, core).
Axes of the slice: x: 2, y: 2, z: 4, core: 2. Of those that a mesh axis runs over, the one named last changes fastest.
Arguments:
- tokens: bfloat16 [4096, 2048], P('dp'), may hold values from -6 to 6
- seq_blocks: int32 [3], replicated, may hold values from 8 to 16, as said below
- block_place: int32 [32], replicated, may hold values from 0 to 31, as said below
- pad_mask: int32 [4096], P('dp'), may hold values from 0 to 1, as said below
- expert_ids: int32 [4096, 8], P('dp'), may hold values from 0 to 63, as said below
- attn_gain: float32 [2048], replicated, may hold values from 0.25 to 1.75
- w_qkv: bfloat16 [2048, 3, 2048], P(None, None, 'tensor'), may hold values from -0.125 to 0.125
- qk_gain: float32 [2, 2048], P(None, 'tensor'), may hold values from 0.25 to 1.75
- w_out: bfloat16 [2048, 2048], P('tensor'), may hold values from -1 to 1
- ffn_gain: float32 [2048], replicated, may hold values from 0.25 to 1.75
- router: bfloat16 [2048, 64], replicated, may hold values from -0.15625 to 0.15625
- expert_in: bfloat16 [2, 2048, 2, 1024], P(None, None, None, 'tensor'), may hold values from -0.125 to 0.125
- expert_out: bfloat16 [2, 1024, 2048], P(None, 'tensor'), may hold values from -16 to 16
- cotangent: bfloat16 [4096, 2048], P('dp', 'tensor'), may hold values from -6 to 6
Outputs:
- output: bfloat16 [4096, 2048], P('dp', 'tensor')
- input_grad: bfloat16 [4096, 2048], P('dp', 'tensor')
- grad_attn_gain: float32 [2048], P('tensor')
- grad_qkv: float32 [2048, 3, 2048], P(None, None, 'tensor')
- grad_qk_gain: float32 [2, 2048], P(None, 'tensor')
- grad_out: float32 [2048, 2048], P('tensor')
- grad_ffn_gain: float32 [2048], P('tensor')
- grad_router: float32 [2048, 64], P('tensor')
- grad_expert_in: float32 [2, 2048, 2, 1024], P(None, None, None, 'tensor')
- grad_expert_out: float32 [2, 1024, 2048], P(None, 'tensor')
Inputs may be any that keep to these rules, and one draw needn't show every extreme that they name: `seq_blocks`: they sum to 32; each is at least 8; the largest is exactly 16. A permutation: rows b * 128 to (b + 1) * 128 - 1 of the given order are packed block block_place[b]. `pad_mask`: zeros only at the end of each sequence, in its last two packed blocks: from 128 to 255 of its last tokens. `expert_ids`: each row names 8 different experts; in the rows of one index of dp (aligned blocks of 512 rows) each expert below 2 is named by at most 128 rows, and by exactly 128 rows in some block.
All inputs are finite; a program needn't handle non-finite values.
Results may differ from a plain program's by a relative error of at most 0.029.
Values may be sent and summed in bfloat16 or wider, within the bound.
A program may use at most 384 MiB of HBM per device.

v0:
```python
import jax
import jax.numpy as jnp
from jax import lax
from jax.sharding import PartitionSpec as P

HDIM = 128
WIN = 2
BLOCK = 128
CAP = 128


EPSILON = 1e-05
ROPE_BASE = 10000.0
NEGATIVE = -1e30


def row_scale(values):
    return lax.rsqrt(jnp.mean(values * values, axis=-1, keepdims=True) + EPSILON)


def rotate(values, positions):
    half_dim = values.shape[-1] // 2
    inv_freq = ROPE_BASE ** (-(jnp.arange(half_dim, dtype=jnp.float32) * 2.0) / values.shape[-1])
    turn_angle = positions.astype(jnp.float32)[:, None] * inv_freq[None, :]
    cosine = jnp.cos(turn_angle)[:, None, :]
    sine_vals = jnp.sin(turn_angle)[:, None, :]
    first_half = values[..., :half_dim]
    second_half = values[..., half_dim:]
    return jnp.concatenate(
        [
            first_half * cosine - second_half * sine_vals,
            second_half * cosine + first_half * sine_vals,
        ],
        axis=-1,
    )


def token_tables(seq_blocks, block_place, row_ids):
    block_total = block_place.shape[0]
    seq_total = seq_blocks.shape[0]
    seq_ends = jnp.cumsum(seq_blocks)
    seq_firsts = seq_ends - seq_blocks
    given_block = row_ids // BLOCK
    packed = jnp.sum(
        jnp.where(
            given_block[:, None] == jnp.arange(block_total, dtype=jnp.int32)[None, :],
            block_place[None, :],
            0,
        ),
        axis=1,
    )
    seq_of = jnp.sum((packed[:, None] >= seq_ends[None, :]).astype(jnp.int32), axis=1)
    first_of = jnp.sum(
        jnp.where(
            seq_of[:, None] == jnp.arange(seq_total, dtype=jnp.int32)[None, :],
            seq_firsts[None, :],
            0,
        ),
        axis=1,
    )
    return (seq_of, (packed - first_of) * BLOCK + row_ids % BLOCK)


def norm_back(values, row_factor, gain_row, incoming, model_width):
    scaled = gain_row * incoming
    inner_sum = jnp.sum(scaled * values, axis=-1, keepdims=True)
    return row_factor * scaled - values * (row_factor**3 / model_width) * inner_sum


def masked_scores(query_rows, seg_rows, pos_rows, key_rows, seg_cols, pos_cols, keep_cols):
    raw_scores = jnp.einsum(
        "qhd,khd->hqk", query_rows, key_rows, preferred_element_type=jnp.float32
    )
    allowed = (
        (seg_rows[:, None] == seg_cols[None, :])
        & (pos_cols[None, :] <= pos_rows[:, None])
        & (keep_cols[None, :] > 0)
    )
    return jnp.where(allowed[None], raw_scores * HDIM ** (-0.5), NEGATIVE)


def score_grads(
    query_rows,
    seg_rows,
    pos_rows,
    top_rows,
    shift_rows,
    du_rows,
    key_rows,
    value_rows,
    seg_cols,
    pos_cols,
    keep_cols,
):
    weights = jnp.exp(
        masked_scores(query_rows, seg_rows, pos_rows, key_rows, seg_cols, pos_cols, keep_cols)
        - top_rows[:, :, None]
    )
    value_dots = jnp.einsum("qhd,khd->hqk", du_rows, value_rows, preferred_element_type=jnp.float32)
    score_grad = (weights * (value_dots - shift_rows[:, :, None]) * HDIM ** (-0.5)).astype(
        jnp.bfloat16
    )
    return (weights.astype(jnp.bfloat16), score_grad)


def body(
    tokens,
    seq_blocks,
    block_place,
    pad_mask,
    expert_ids,
    attn_gain,
    w_qkv,
    qk_gain,
    w_out,
    ffn_gain,
    router,
    expert_in,
    expert_out,
    cotangent,
):
    rows_here = tokens.shape[0]
    model_width = tokens.shape[1]
    local_width = w_qkv.shape[2]
    heads_here = local_width // HDIM
    local_ff = expert_out.shape[1]
    tensor_index = lax.axis_index("tensor")
    feature_start = tensor_index * local_width
    first_row = lax.axis_index("dp") * rows_here
    row_ids = first_row + jnp.arange(rows_here, dtype=jnp.int32)
    seg_q, pos_q = token_tables(seq_blocks, block_place, row_ids)
    inputs = tokens.astype(jnp.float32)
    x_scale = row_scale(inputs)
    normed_in = (inputs * x_scale * attn_gain).astype(jnp.bfloat16)
    projected = jnp.dot(
        normed_in, w_qkv.reshape(model_width, 3 * local_width), preferred_element_type=jnp.float32
    ).reshape(rows_here, 3, local_width)
    queries = projected[:, 0]
    keys_here = projected[:, 1]
    values_here = projected[:, 2]
    sums_q, sums_k = lax.psum(
        (jnp.sum(queries * queries, axis=-1), jnp.sum(keys_here * keys_here, axis=-1)), "tensor"
    )
    q_scale = lax.rsqrt(sums_q / model_width + EPSILON)[:, None]
    k_scale = lax.rsqrt(sums_k / model_width + EPSILON)[:, None]
    q_norm = (queries * q_scale * qk_gain[0]).reshape(rows_here, heads_here, HDIM)
    k_norm = (keys_here * k_scale * qk_gain[1]).reshape(rows_here, heads_here, HDIM)
    q_rot = rotate(q_norm, pos_q).astype(jnp.bfloat16)
    k_rot = rotate(k_norm, pos_q).astype(jnp.bfloat16)
    v_low = values_here.astype(jnp.bfloat16)
    keep_here = pad_mask.astype(jnp.bfloat16)
    k_all, v_all, keep_all = (
        lax.all_gather(k_rot.reshape(rows_here, local_width), "dp", axis=0, tiled=True),
        lax.all_gather(v_low, "dp", axis=0, tiled=True),
        lax.all_gather(keep_here, "dp", axis=0, tiled=True),
    )
    total_rows = k_all.shape[0]
    all_ids = jnp.arange(total_rows, dtype=jnp.int32)
    seg_keys, pos_keys = token_tables(seq_blocks, block_place, all_ids)
    key_block = min(1024, total_rows)
    block_count = total_rows // key_block
    keys_blocks = k_all.reshape(block_count, key_block, heads_here, HDIM)
    values_blocks = v_all.reshape(block_count, key_block, heads_here, HDIM)
    seg_blocks = seg_keys.reshape(block_count, key_block)
    pos_blocks = pos_keys.reshape(block_count, key_block)
    keep_blocks = keep_all.reshape(block_count, key_block)

    def online_step(carry_state, block_in):
        run_top, row_acc, value_acc = carry_state
        keys_b, values_b, seg_b, pos_b, keep_b = block_in
        found = masked_scores(q_rot, seg_q, pos_q, keys_b, seg_b, pos_b, keep_b)
        new_top = jnp.maximum(run_top, jnp.max(found, axis=-1))
        factor = jnp.exp(run_top - new_top)
        weights = jnp.exp(found - new_top[:, :, None])
        row_acc = row_acc * factor + jnp.sum(weights, axis=-1)
        value_acc = value_acc * jnp.transpose(factor)[:, :, None] + jnp.einsum(
            "hqk,khd->qhd",
            weights.astype(jnp.bfloat16),
            values_b,
            preferred_element_type=jnp.float32,
        )
        return ((new_top, row_acc, value_acc), None)

    start_state = (
        jnp.full((heads_here, rows_here), NEGATIVE, jnp.float32),
        jnp.zeros((heads_here, rows_here), jnp.float32),
        jnp.zeros((rows_here, heads_here, HDIM), jnp.float32),
    )
    (row_top, row_sum, value_sum), _ = lax.scan(
        online_step, start_state, (keys_blocks, values_blocks, seg_blocks, pos_blocks, keep_blocks)
    )
    attended = value_sum / jnp.transpose(row_sum)[:, :, None]
    attended_low = attended.astype(jnp.bfloat16).reshape(rows_here, local_width)
    branch = lax.psum(
        jnp.dot(attended_low, w_out, preferred_element_type=jnp.float32).astype(jnp.bfloat16),
        "tensor",
    ).astype(jnp.float32)
    hidden = inputs + branch
    h_scale = row_scale(hidden)
    normed = (hidden * h_scale * ffn_gain).astype(jnp.bfloat16)
    logits = jnp.dot(normed, router, preferred_element_type=jnp.float32)
    router_probs = jax.nn.softmax(logits, axis=-1)
    window_ids = jnp.arange(WIN, dtype=jnp.int32)
    chosen = jnp.any(expert_ids[:, :, None] == window_ids[None, None, :], axis=1)
    chosen_float = chosen.astype(jnp.float32)
    gate_values = router_probs[:, :WIN] * chosen_float
    slot_ids = jnp.arange(CAP, dtype=jnp.int32)
    token_ids = jnp.arange(rows_here, dtype=jnp.int32)
    mixture = jnp.zeros((rows_here, model_width), jnp.float32)
    saved_slots = []
    for expert in range(WIN):
        picked = chosen[:, expert]
        slot_rank = jnp.cumsum(picked.astype(jnp.int32)) - 1
        slot_table = (slot_rank[None, :] == slot_ids[:, None]) & picked[None, :]
        slot_token = jnp.sum(jnp.where(slot_table, token_ids[None, :], 0), axis=1)
        slot_live = jnp.any(slot_table, axis=1).astype(jnp.float32)
        gathered_rows = jnp.take(normed, slot_token, axis=0)
        gate_up = jnp.dot(
            gathered_rows,
            expert_in[expert].reshape(model_width, 2 * local_ff),
            preferred_element_type=jnp.float32,
        ).reshape(CAP, 2, local_ff)
        active = (jax.nn.silu(gate_up[:, 0]) * gate_up[:, 1]).astype(jnp.bfloat16)
        expert_part = jnp.dot(active, expert_out[expert], preferred_element_type=jnp.float32)
        slot_gate = jnp.take(gate_values[:, expert], slot_token) * slot_live
        mixture = mixture.at[slot_token].add(slot_gate[:, None] * expert_part)
        saved_slots.append(
            (slot_token, slot_live, gathered_rows, gate_up, active, expert_part, slot_gate)
        )
    mixture_share = lax.psum_scatter(
        mixture.astype(jnp.bfloat16), "tensor", scatter_dimension=1, tiled=True
    ).astype(jnp.float32)
    hidden_share = lax.dynamic_slice_in_dim(hidden, feature_start, local_width, 1)
    output = (hidden_share + mixture_share).astype(jnp.bfloat16)
    cot_full = lax.all_gather(cotangent, "tensor", axis=1, tiled=True).astype(jnp.float32)
    mixture_grad = jnp.zeros((rows_here, model_width), jnp.float32)
    gate_columns = []
    expert_in_list = []
    expert_out_list = []
    for expert in range(WIN):
        slot_token, slot_live, gathered_rows, gate_up, active, expert_part, slot_gate = saved_slots[
            expert
        ]
        cot_rows = jnp.take(cot_full, slot_token, axis=0)
        part_grad = (slot_gate[:, None] * cot_rows).astype(jnp.bfloat16)
        slot_dots = jnp.sum(cot_rows * expert_part, axis=-1) * slot_live
        gate_columns.append(jnp.zeros((rows_here,), jnp.float32).at[slot_token].add(slot_dots))
        expert_out_list.append(
            jnp.einsum("cf,cd->fd", active, part_grad, preferred_element_type=jnp.float32)
        )
        active_grad = jnp.einsum(
            "cd,fd->cf", part_grad, expert_out[expert], preferred_element_type=jnp.float32
        )
        _, silu_pull = jax.vjp(
            lambda gate_in, up_in: jax.nn.silu(gate_in) * up_in, gate_up[:, 0], gate_up[:, 1]
        )
        gate_in_grad, up_in_grad = silu_pull(active_grad)
        pair_grad = (
            jnp.stack([gate_in_grad, up_in_grad], axis=1)
            .astype(jnp.bfloat16)
            .reshape(CAP, 2 * local_ff)
        )
        expert_in_list.append(
            jnp.einsum(
                "cd,cf->df", gathered_rows, pair_grad, preferred_element_type=jnp.float32
            ).reshape(model_width, 2, local_ff)
        )
        row_grad = jnp.einsum(
            "cf,df->cd",
            pair_grad,
            expert_in[expert].reshape(model_width, 2 * local_ff),
            preferred_element_type=jnp.float32,
        )
        mixture_grad = mixture_grad.at[slot_token].add(row_grad)
    gate_grad = jnp.stack(gate_columns, axis=1)
    mixture_grad, gate_grad = (
        lax.psum(mixture_grad.astype(jnp.bfloat16), "tensor").astype(jnp.float32),
        lax.psum(gate_grad.astype(jnp.bfloat16), "tensor").astype(jnp.float32),
    )
    probs_grad = jnp.concatenate(
        [gate_grad * chosen_float, jnp.zeros((rows_here, router.shape[1] - WIN), jnp.float32)],
        axis=1,
    )
    logit_grad = (
        router_probs * (probs_grad - jnp.sum(router_probs * probs_grad, axis=-1, keepdims=True))
    ).astype(jnp.bfloat16)
    normed_grad = mixture_grad + jnp.einsum(
        "te,de->td", logit_grad, router, preferred_element_type=jnp.float32
    )
    normed_share = lax.dynamic_slice_in_dim(normed, feature_start, local_width, 1)
    router_grad = jnp.einsum(
        "td,te->de", normed_share, logit_grad, preferred_element_type=jnp.float32
    )
    ffn_gain_grad = lax.dynamic_slice_in_dim(
        jnp.sum(normed_grad * hidden * h_scale, axis=0), feature_start, local_width, 0
    )
    hidden_grad = cot_full + norm_back(hidden, h_scale, ffn_gain, normed_grad, model_width)
    expert_in_grad = jnp.stack(expert_in_list)
    expert_out_grad = jnp.stack(expert_out_list)
    branch_grad = hidden_grad.astype(jnp.bfloat16)
    out_grad = jnp.einsum(
        "tc,td->cd", attended_low, branch_grad, preferred_element_type=jnp.float32
    )
    attended_grad = (
        jnp.einsum("td,cd->tc", branch_grad, w_out, preferred_element_type=jnp.float32)
        .astype(jnp.bfloat16)
        .reshape(rows_here, heads_here, HDIM)
    )
    grad_wide = attended_grad.astype(jnp.float32)
    delta_rows = jnp.transpose(jnp.sum(grad_wide * attended, axis=-1))
    scaled_grad = (grad_wide / jnp.transpose(row_sum)[:, :, None]).astype(jnp.bfloat16)
    shift_rows = delta_rows / row_sum

    def key_step(carry_sum, block_in):
        keys_b, values_b, seg_b, pos_b, keep_b = block_in
        low_weights, score_grad = score_grads(
            q_rot,
            seg_q,
            pos_q,
            row_top,
            shift_rows,
            scaled_grad,
            keys_b,
            values_b,
            seg_b,
            pos_b,
            keep_b,
        )
        carry_sum = carry_sum + jnp.einsum(
            "hqk,khd->qhd", score_grad, keys_b, preferred_element_type=jnp.float32
        )
        key_term = jnp.einsum("hqk,qhd->khd", score_grad, q_rot, preferred_element_type=jnp.float32)
        value_term = jnp.einsum(
            "hqk,qhd->khd", low_weights, scaled_grad, preferred_element_type=jnp.float32
        )
        return (
            carry_sum,
            jnp.concatenate(
                [
                    key_term.reshape(key_block, local_width),
                    value_term.reshape(key_block, local_width),
                ],
                axis=1,
            ),
        )

    query_grad, kv_terms = lax.scan(
        key_step,
        jnp.zeros((rows_here, heads_here, HDIM), jnp.float32),
        (keys_blocks, values_blocks, seg_blocks, pos_blocks, keep_blocks),
    )
    kv_grad = lax.psum_scatter(
        kv_terms.reshape(total_rows, 2 * local_width).astype(jnp.bfloat16),
        "dp",
        scatter_dimension=0,
        tiled=True,
    ).astype(jnp.float32)
    key_grad = kv_grad[:, :local_width]
    value_grad = kv_grad[:, local_width:]
    value_low_grad = value_grad.astype(jnp.bfloat16)
    _, rope_pull = jax.vjp(lambda turned: rotate(turned, pos_q), q_norm)
    q_norm_grad = rope_pull(query_grad)[0].reshape(rows_here, local_width)
    k_norm_grad = rope_pull(key_grad.reshape(rows_here, heads_here, HDIM))[0].reshape(
        rows_here, local_width
    )
    scaled_q = qk_gain[0] * q_norm_grad
    scaled_k = qk_gain[1] * k_norm_grad
    inner_q, inner_k = lax.psum(
        (jnp.sum(scaled_q * queries, axis=-1), jnp.sum(scaled_k * keys_here, axis=-1)), "tensor"
    )
    q_grad = (
        q_scale * scaled_q - queries * (q_scale**3 / model_width) * inner_q[:, None]
    ).astype(jnp.bfloat16)
    k_grad = (
        k_scale * scaled_k - keys_here * (k_scale**3 / model_width) * inner_k[:, None]
    ).astype(jnp.bfloat16)
    qk_gain_grad = jnp.stack(
        [
            jnp.sum(q_norm_grad * queries * q_scale, axis=0),
            jnp.sum(k_norm_grad * keys_here * k_scale, axis=0),
        ]
    )
    proj_grad = jnp.stack([q_grad, k_grad, value_low_grad], axis=1).reshape(
        rows_here, 3 * local_width
    )
    qkv_grad = jnp.einsum(
        "td,tc->dc", normed_in, proj_grad, preferred_element_type=jnp.float32
    ).reshape(model_width, 3, local_width)
    normed_in_grad = jnp.einsum(
        "tc,dc->td",
        proj_grad,
        w_qkv.reshape(model_width, 3 * local_width),
        preferred_element_type=jnp.float32,
    )
    input_part = norm_back(inputs, x_scale, attn_gain, normed_in_grad, model_width)
    gain_part = jnp.sum(normed_in_grad * inputs * x_scale, axis=0)
    input_sum, attn_gain_grad = (
        lax.psum_scatter(
            input_part.astype(jnp.bfloat16), "tensor", scatter_dimension=1, tiled=True
        ).astype(jnp.float32),
        lax.psum_scatter(
            gain_part.astype(jnp.bfloat16), "tensor", scatter_dimension=0, tiled=True
        ).astype(jnp.float32),
    )
    input_grad = (
        lax.dynamic_slice_in_dim(hidden_grad, feature_start, local_width, 1) + input_sum
    ).astype(jnp.bfloat16)
    (
        attn_gain_grad,
        qkv_grad,
        qk_gain_grad,
        out_grad,
        ffn_gain_grad,
        router_grad,
        expert_in_grad,
        expert_out_grad,
    ) = (
        lax.psum(attn_gain_grad.astype(jnp.bfloat16), "dp").astype(jnp.float32),
        lax.psum(qkv_grad.astype(jnp.bfloat16), "dp").astype(jnp.float32),
        lax.psum(qk_gain_grad.astype(jnp.bfloat16), "dp").astype(jnp.float32),
        lax.psum(out_grad.astype(jnp.bfloat16), "dp").astype(jnp.float32),
        lax.psum(ffn_gain_grad.astype(jnp.bfloat16), "dp").astype(jnp.float32),
        lax.psum(router_grad.astype(jnp.bfloat16), "dp").astype(jnp.float32),
        lax.psum(expert_in_grad.astype(jnp.bfloat16), "dp").astype(jnp.float32),
        lax.psum(expert_out_grad.astype(jnp.bfloat16), "dp").astype(jnp.float32),
    )
    return (
        output,
        input_grad,
        attn_gain_grad,
        qkv_grad,
        qk_gain_grad,
        out_grad,
        ffn_gain_grad,
        router_grad,
        expert_in_grad,
        expert_out_grad,
    )


def solution(mesh):
    placed = (
        P("dp", None),
        P(),
        P(),
        P("dp"),
        P("dp", None),
        P(),
        P(None, None, "tensor"),
        P(None, "tensor"),
        P("tensor", None),
        P(),
        P(),
        P(None, None, None, "tensor"),
        P(None, "tensor", None),
        P("dp", "tensor"),
    )
    return jax.shard_map(
        body,
        mesh=mesh,
        in_specs=placed,
        out_specs=(
            P("dp", "tensor"),
            P("dp", "tensor"),
            P("tensor"),
            P(None, None, "tensor"),
            P(None, "tensor"),
            P("tensor", None),
            P("tensor"),
            P("tensor", None),
            P(None, None, None, "tensor"),
            P(None, "tensor", None),
        ),
        check_vma=False,
    )
```

profile of v0, /device:TPU:0, one launch (start us, length us, event | category | flops | bytes accessed | tf_op | source)
XLA Modules:
  0.0 1285.8 jit_solution(6470624476865635118)
XLA Ops:
  7.3 8.9 copy.125
  18.8 6.4 fusion.48
  27.9 8.4 all-reduce.7
  46.3 6.2 fusion.180
  52.5 27.1 %all-gather.1 = bf16[8,1,512]{2,1,0:T(2,128)(2,1)S(1)} all-gather(bf16[1,1,512]{2,1,0:T(2,128)(2,1)S(1)} %reshape.852), channel_id=1, replica_groups=mesh['dp'=8,'tensor'=4] {'dp'}, dimensions={0}, use_global_device_ids=true | all-gather | bytes 9216 | tf_op jit(solution)/shard_map/all_gather | solution.py:155
  80.7 34.1 %all-gather.6.cloned.1.call-done = bf16[4096,512]{1,0:T(8,128)(2,1)} async-done(((bf16[512,512]{1,0:T(8,128)(2,1)}), bf16[4096,512]{1,0:T(8,128)(2,1)}) %all-gather.6.cloned.1.call-update) | async-done | bytes 4194320 | tf_op jit(solution)/shard_map/all_gather | solution.py:153
  114.8 6.9 reshape.731
  121.7 5.2 copy.127
  126.9 63.7 %all-gather.10.cloned.1.call-done = bf16[4096,1,512]{0,2,1:T(8,128)(2,1)} async-done(((bf16[512,1,512]{0,2,1:T(8,128)(2,1)}), bf16[4096,1,512]{0,2,1:T(8,128)(2,1)}) %all-gather.10.cloned.1.call-update) | async-done | bytes 4194320 | tf_op jit(solution)/shard_map/all_gather | solution.py:154
  190.6 7.9 reshape.732
  198.5 5.6 copy.129
  204.1 73.0 %while.28 = (s32[]{:T(128)}, f32[4,512]{1,0:T(4,128)S(1)}, f32[4,512]{1,0:T(4,128)S(1)}, f32[512,4,128]{0,2,1:T(8,128)}, s32[512]{0:T(512)S(1)}, /*index=5*/s32[...) while((s32[]{:T(128)}, f32[4,512]{1,0:T(4,128)S(1)}, ...), condition=%wide.region_15.16_spmd.clone, body=%wide.region_12.15_spmd.clone.sunk | while | flops 1099709440 | bytes 65700036 | solution.py:189
  205.1 6.4 fusion.241
  211.5 4.5 fusion.243
  217.3 4.8 fusion.245
  223.1 6.3 fusion.241
  229.5 4.5 fusion.243
  235.3 5.1 fusion.245
  241.5 6.3 fusion.241
  247.8 4.5 fusion.243
  253.6 5.1 fusion.245
  259.8 6.3 fusion.241
  266.1 4.5 fusion.243
  272.0 5.1 fusion.245
  281.5 3.4 copy.157
  284.9 4.0 copy.130
  288.9 3.4 copy.158
  292.2 4.0 copy.131
  296.5 4.2 convert_element_type.254
  300.7 4.6 gather_fusion.4
  305.3 4.6 gather_fusion.5
  309.9 21.3 %all-reduce.14.cloned.1.call-done = bf16[512,2048]{1,0:T(8,128)(2,1)} async-done(((bf16[512,2048]{1,0:T(8,128)(2,1)}), bf16[512,2048]{1,0:T(8,128)(2,1)}) %all-reduce.14.cloned.1.call-update) | async-done | bytes 2097168 | tf_op jit(solution)/shard_map/psum | solution.py:194
  340.6 4.3 gather_fusion.3
  359.5 6.2 psum.109
  374.7 3.5 fusion.191
  378.2 5.1 scatter_custom_fusion.2
  385.5 3.4 fusion.192
  388.9 7.0 scatter_fusion
  395.9 3.8 convert_element_type.261
  400.0 7.9 copy.135
  407.9 43.8 %all-reduce.16.cloned.1.call-done = bf16[512,2048]{1,0:T(8,128)(2,1)} async-done(((bf16[512,2048]{1,0:T(8,128)(2,1)}), bf16[512,2048]{1,0:T(8,128)(2,1)}) %all-reduce.16.cloned.1.call-update) | async-done | bytes 2097168 | tf_op jit(solution)/shard_map/psum | solution.py:277
  451.8 5.4 multiply_reduce_fusion
  462.7 87.2 %while.29 = (s32[]{:T(128)}, f32[512,4,128]{0,2,1:T(8,128)}, bf16[4,1024,1024]{1,2,0:T(8,128)(2,1)}, bf16[4,1024,4,128]{3,1,2,0:T(8,128)(2,1)}, s32[512]{0:T(512...) while((s32[]{:T(128)}, f32[512,4,128]{0,2,1:T(8,128)}, ...), condition=%wide.region_44.48_spmd.clone, body=%wide.region_43.47_spmd.clone.sunk | while | flops 2714242048 | bytes 145285456 | solution.py:347
  467.0 6.5 fusion.257
  473.5 3.7 fusion.258
  488.8 6.5 fusion.257
  495.3 3.6 fusion.258
  510.6 6.5 fusion.257
  517.1 3.6 fusion.258
  532.3 6.5 fusion.257
  538.8 3.6 fusion.258
  550.0 8.2 copy.156
  559.4 4.6 scatter_custom_fusion
  564.1 7.2 scatter_custom_fusion.1
  571.3 3.8 convert_element_type.251
  575.2 131.2 %reduce-scatter.6.cloned.1.call-done = bf16[512,1024]{0,1:T(8,128)(2,1)} async-done(((bf16[4096,1024]{0,1:T(8,128)(2,1)}), bf16[512,1024]{0,1:T(8,128)(2,1)}) %reduce-scatter.6.cloned.1.call-update) | async-done | bytes 1048592 | tf_op jit(solution)/shard_map/reduce_scatter | solution.py:352
  712.9 6.7 all-reduce.6
  722.1 7.9 fusion.58
  748.5 6.0 convolution_convert_fusion
  759.5 6.9 all-reduce.5
  766.5 19.5 %all-reduce.8 = (bf16[512]{0:T(512)(128)(2,1)S(1)}, bf16[2,512]{1,0:T(2,128)(2,1)S(1)}, bf16[512]{0:T(512)(128)(2,1)S(1)}) all-reduce(bf16[512]{0:T(512)(128)(2,1)S(1)} %dynamic-slice.1, bf16[2,512]{1,0:T(2,128)(2,1)S(1)} %pad_maximum_fusion.8, bf16[512]{0:T(512)(128)(2,1)S(1)} %dynamic_slice.102), channel_id=1, replica_groups=mesh['dp'=8,'tensor'=4] {'dp'}, use_global_device_ids=true, to_apply=%region_54.58 | all-reduce | flops 2048 | bytes 8192 | tf_op jit(solution)/shard_map/psum | solution.py:418
  790.1 446.2 %all-reduce.18.cloned.1.call-done = (bf16[2,2048,2,256]{3,1,2,0:T(8,128)(2,1)}, bf16[2048,3,512]{2,0,1:T(8,128)(2,1)}, bf16[512,2048]{1,0:T(8,128)(2,1)}, bf16[512,64]{0,1:T(8,128)(2,1)}, bf16[2,256,2048]{2,1,0:T(8,128)(2,1)}) async-done(((bf16[2,2048,2,256]{3,1,2,0:T(8,128)(2,1)}, bf16[2048,3,512]{2,0,1:T(8,128)(2,1)}, bf16[512,2048]{1,0:T(8,128)(2,1)}, bf16[512,64]{0,1:T(8,128)(2,1)}, ...) | async-done | bytes 14745616 | tf_op jit(solution)/shard_map/psum | solution.py:424
  1236.3 9.5 convert_element_type.280
  1249.6 26.9 %copy.141 = f32[2,2048,2,256]{3,2,1,0:T(2,128)} copy(bf16[2,2048,2,256]{3,1,2,0:T(8,128)(2,1)S(1)} %copy-done.25) | data formatting | bytes 12582912
  (472 shorter events, 160.0 us)
Async XLA Ops:
  7.2 271.3 %copy-start = (bf16[512,2048]{1,0:T(8,128)(2,1)S(1)}, bf16[512,2048]{1,0:T(8,128)(2,1)}, u32[]{:S(2)}) copy-start(bf16[512,2048]{1,0:T(8,128)(2,1)} %param.32) | copy-start | bytes 6291460
  7.2 107.6 %all-gather.6.cloned.1.call-start = ((), (), s32[]{:S(2)}) async-start(), calls=%async_computation.3 | async-start | bytes 4718592 | tf_op jit(solution)/shard_map/all_gather | solution.py:153
  7.2 11.6 copy-start.78
  18.8 6.4 copy-start.82
  27.2 13.0 %copy-start.19 = (f32[512,1,512]{0,2,1:T(8,128)}, f32[512,1,512]{0,2,1:T(8,128)S(1)}, u32[]{:S(2)}) copy-start(f32[512,1,512]{0,2,1:T(8,128)S(1)} %get-tuple-element.512) | copy-start | bytes 3145732
  27.9 12.3 copy-start.65
  27.9 12.3 copy-start.67
  41.3 149.3 %all-gather.10.cloned.1.call-start = ((), (), s32[]{:S(2)}) async-start(), calls=%async_computation.10 | async-start | bytes 4718592 | tf_op jit(solution)/shard_map/all_gather | solution.py:154
  43.5 253.1 %all-gather.8.cloned.1.call-start = ((), (), s32[]{:S(2)}) async-start(), calls=%async_computation.6 | async-start | bytes 2621440 | tf_op jit(solution)/shard_map/all_gather | solution.py:235
  44.2 287.0 %all-reduce.14.cloned.1.call-start = ((), (), s32[]{:S(2)}) async-start(), calls=%async_computation.4 | async-start | bytes 4194304 | tf_op jit(solution)/shard_map/psum | solution.py:194
  44.7 321.0 %copy-start.60 = (pred[512,2]{0,1:T(4,128)(4,1)}, pred[512,2]{0,1:T(4,128)(4,1)S(1)}, u32[]{:S(2)}) copy-start(pred[512,2]{0,1:T(4,128)(4,1)S(1)} %fusion.142) | copy-start | bytes 3076
  46.2 250.2 %copy-start.106 = (s32[128]{0:T(128)}, s32[128]{0:T(128)S(1)}, u32[]{:S(2)}) copy-start(s32[128]{0:T(128)S(1)} %get-tuple-element.562) | copy-start | bytes 1540
  46.2 250.3 %copy-start.104 = (s32[128]{0:T(128)}, s32[128]{0:T(128)S(1)}, u32[]{:S(2)}) copy-start(s32[128]{0:T(128)S(1)} %get-tuple-element.561) | copy-start | bytes 1540
  46.2 291.1 %copy-start.92 = (s32[1024]{0:T(1024)}, s32[1024]{0:T(1024)S(1)}, u32[]{:S(2)}) copy-start(s32[1024]{0:T(1024)S(1)} %pad_clamp_fusion.1) | copy-start | bytes 12292
  46.2 33.4 %copy-start.41 = (bf16[512,4,64]{0,2,1:T(8,128)(2,1)S(1)}, bf16[512,4,64]{0,2,1:T(8,128)(2,1)}, u32[]{:S(2)}) copy-start(bf16[512,4,64]{0,2,1:T(8,128)(2,1)} %get-tuple-element.518) | copy-start | bytes 786436
  281.2 170.6 %all-reduce.16.cloned.1.call-start = ((), (), s32[]{:S(2)}) async-start(), calls=%async_computation.7 | async-start | bytes 4194304 | tf_op jit(solution)/shard_map/psum | solution.py:277
  281.5 59.1 %copy-start.93 = (s32[1024]{0:T(1024)}, s32[1024]{0:T(1024)S(1)}, u32[]{:S(2)}) copy-start(s32[1024]{0:T(1024)S(1)} %pad_clamp_fusion) | copy-start | bytes 12292
  296.4 54.1 %copy-start.108 = (pred[128]{0:T(512)(128)(4,1)}, pred[128]{0:T(512)(128)(4,1)S(1)}, u32[]{:S(2)}) copy-start(pred[128]{0:T(512)(128)(4,1)S(1)} %get-tuple-element.564) | copy-start | bytes 388
  296.4 61.6 %copy-start.110 = (pred[128]{0:T(512)(128)(4,1)}, pred[128]{0:T(512)(128)(4,1)S(1)}, u32[]{:S(2)}) copy-start(pred[128]{0:T(512)(128)(4,1)S(1)} %get-tuple-element.563) | copy-start | bytes 388
  296.4 61.6 %copy-start.114 = (s32[128]{0:T(128)}, s32[128]{0:T(128)S(1)}, u32[]{:S(2)}) copy-start(s32[128]{0:T(128)S(1)} %fusion.163) | copy-start | bytes 1540
  296.4 58.0 %copy-start.87 = (pred[128]{0:T(512)(128)(4,1)}, pred[128]{0:T(512)(128)(4,1)S(1)}, u32[]{:S(2)}) copy-start(pred[128]{0:T(512)(128)(4,1)S(1)} %compare_and_fusion.1) | copy-start | bytes 388
  296.5 54.0 %copy-start.111 = (s32[128]{0:T(128)}, s32[128]{0:T(128)S(1)}, u32[]{:S(2)}) copy-start(s32[128]{0:T(128)S(1)} %fusion.164) | copy-start | bytes 1540
  296.5 51.0 %copy-start.89 = (pred[128]{0:T(512)(128)(4,1)}, pred[128]{0:T(512)(128)(4,1)S(1)}, u32[]{:S(2)}) copy-start(pred[128]{0:T(512)(128)(4,1)S(1)} %compare_and_fusion) | copy-start | bytes 388
  309.9 25.0 %copy-start.63 = (f32[2048]{0:T(1024)S(1)}, f32[2048]{0:T(1024)}, u32[]{:S(2)}) copy-start(f32[2048]{0:T(1024)} %param.33) | copy-start | bytes 24580
  340.6 11.4 copy-start.24
  347.5 35.7 %copy-start.37 = (f32[128,2,256]{2,0,1:T(8,128)}, f32[128,2,256]{2,0,1:T(8,128)S(1)}, u32[]{:S(2)}) copy-start(f32[128,2,256]{2,0,1:T(8,128)S(1)} %fusion.104) | copy-start | bytes 786436
  355.1 15.2 %copy-start.107 = (s32[128]{0:T(128)S(1)}, s32[128]{0:T(128)}, u32[]{:S(2)}) copy-start(s32[128]{0:T(128)} %copy-done.106) | copy-start | bytes 1540
  355.1 17.3 %copy-start.105 = (s32[128]{0:T(128)S(1)}, s32[128]{0:T(128)}, u32[]{:S(2)}) copy-start(s32[128]{0:T(128)} %copy-done.104) | copy-start | bytes 1540
  355.1 17.3 %copy-start.109 = (pred[128]{0:T(512)(128)(4,1)S(1)}, pred[128]{0:T(512)(128)(4,1)}, u32[]{:S(2)}) copy-start(pred[128]{0:T(512)(128)(4,1)} %copy-done.108) | copy-start | bytes 388
  365.7 86.0 %copy-start.61 = (f32[512,2]{0,1:T(2,128)}, f32[512,2]{0,1:T(2,128)S(1)}, u32[]{:S(2)}) copy-start(f32[512,2]{0,1:T(2,128)S(1)} %convert_select_fusion) | copy-start | bytes 12292
  368.2 83.6 %copy-start.80 = (f32[512]{0:T(512)}, f32[512]{0:T(512)S(1)}, u32[]{:S(2)}) copy-start(f32[512]{0:T(512)S(1)} %get-tuple-element.495) | copy-start | bytes 6148
  372.4 10.8 copy-start.96
  374.6 8.7 copy-start.90
  374.7 10.6 copy-start.31
  399.7 306.7 %reduce-scatter.6.cloned.1.call-start = ((), (), s32[]{:S(2)}) async-start(), calls=%async_computation.8 | async-start | bytes 9437184 | tf_op jit(solution)/shard_map/reduce_scatter | solution.py:352
  399.9 51.8 %copy-start.54 = (bf16[2048,64]{0,1:T(8,128)(2,1)S(1)}, bf16[2048,64]{0,1:T(8,128)(2,1)}, u32[]{:S(2)}) copy-start(bf16[2048,64]{0,1:T(8,128)(2,1)} %param.34) | copy-start | bytes 786436
  400.0 51.8 %copy-start.64 = (f32[2048]{0:T(1024)S(1)}, f32[2048]{0:T(1024)}, u32[]{:S(2)}) copy-start(f32[2048]{0:T(1024)} %param.33) | copy-start | bytes 24580
  400.0 51.8 %copy-start.74 = (f32[512]{0:T(512)S(1)}, f32[512]{0:T(512)}, u32[]{:S(2)}) copy-start(f32[512]{0:T(512)} %copy-done.73) | copy-start | bytes 6148
  465.2 8.3 copy-start.4
  467.0 6.5 copy-start.6
  486.9 8.3 copy-start.4
  488.8 6.5 copy-start.6
  508.7 8.3 copy-start.4
  510.5 6.5 copy-start.6
  530.5 8.3 copy-start.4
  532.3 6.5 copy-start.6
  558.3 198.8 %reduce-scatter.4.cloned.1.call-start = ((), (), s32[]{:S(2)}) async-start(), calls=%async_computation.5 | async-start | bytes 2621440 | tf_op jit(solution)/shard_map/reduce_scatter | solution.py:230
  575.1 133.5 %copy-start.8 = (f32[512,4,128]{0,2,1:T(8,128)S(1)}, f32[512,4,128]{0,2,1:T(8,128)}, u32[]{:S(2)}) copy-start(f32[512,4,128]{0,2,1:T(8,128)} %get-tuple-element.153) | copy-start | bytes 3145732
  575.1 133.5 %copy-start.34 = (f32[512,64]{0,1:T(8,128)S(1)}, f32[512,64]{0,1:T(8,128)}, u32[]{:S(2)}) copy-start(f32[512,64]{0,1:T(8,128)} %copy-done.33) | copy-start | bytes 393220
  575.1 133.5 %copy-start.36 = (f32[512,64]{0,1:T(8,128)S(1)}, f32[512,64]{0,1:T(8,128)}, u32[]{:S(2)}) copy-start(f32[512,64]{0,1:T(8,128)} %copy-done.35) | copy-start | bytes 393220
  575.1 133.9 %copy-start.70 = (f32[512]{0:T(512)S(1)}, f32[512]{0:T(512)}, u32[]{:S(2)}) copy-start(f32[512]{0:T(512)} %copy-done.69) | copy-start | bytes 6148
  575.1 212.6 %reduce-scatter.8.cloned.1.call-start = ((), (), s32[]{:S(2)}) async-start(), calls=%async_computation.9 | async-start | bytes 2621440 | tf_op jit(solution)/shard_map/reduce_scatter | solution.py:398
  711.2 8.5 copy-start.76
  711.2 8.5 copy-start.77
  712.0 10.1 copy-start.11
  712.0 10.1 copy-start.79
  712.0 10.1 copy-start.83
  722.0 8.0 copy-start.44
  722.0 8.0 copy-start.46
  722.1 7.9 copy-start.85
  732.3 504.0 %all-reduce.18.cloned.1.call-start = ((), (), s32[]{:S(2)}) async-start(), calls=%async_computation.11 | async-start | bytes 29491200 | tf_op jit(solution)/shard_map/psum | solution.py:424
  1236.3 9.5 copy-start.30
  1249.6 26.9 %copy-start.29 = (bf16[2,256,2048]{2,1,0:T(8,128)(2,1)S(1)}, bf16[2,256,2048]{2,1,0:T(8,128)(2,1)}, u32[]{:S(2)}) copy-start(bf16[2,256,2048]{2,1,0:T(8,128)(2,1)} %get-tuple-element.492) | copy-start | bytes 6291460
  1249.6 29.5 %copy-start.1 = (bf16[512,2048]{1,0:T(8,128)(2,1)S(1)}, bf16[512,2048]{1,0:T(8,128)(2,1)}, u32[]{:S(2)}) copy-start(bf16[512,2048]{1,0:T(8,128)(2,1)} %param.32) | copy-start | bytes 6291460
  (79 other events, 288.8 us)
Sparse Core Ops, SparseCore 0:
  41.4 73.3 all-gather.5
  117.4 73.1 all-gather.9
  192.2 20.7 all-gather.7
  281.3 49.8 all-reduce.13
  399.8 51.8 all-reduce.15
  558.4 147.9 reduce-scatter.5
  709.5 30.2 reduce-scatter.3
  742.9 31.3 reduce-scatter.7
  780.5 455.7 all-reduce.17
where the time goes:
time: 1290 us
  waiting for transfers between devices  741 us (57%)
  matrix products  177 us (14%)
  local copies, waits for them, and re-layouts  149 us (12%)
  other arithmetic  126 us (10%)
  blocking collectives  74.8 us (6%)
  between operations  16.2 us (1%)
    psum x1, waiting for transfers between devices, body(): lax.psum(expert_in_grad.astype(jnp.bfloat16), 'dp').astype(jnp.float32)  446 us
    reduce_scatter x1, waiting for transfers between devices, body(): lax.psum_scatter(kv_terms.reshape(total_rows, 2 * local_width).astype(jnp...  131 us
    unnamed x233, local copies, waits for them, and re-layouts  69.4 us
    all_gather x1, waiting for transfers between devices, body(): lax.all_gather(v_low, 'dp', axis=0, tiled=True)  63.7 us
    psum x1, waiting for transfers between devices, body(): lax.psum(mixture_grad.astype(jnp.bfloat16), 'tensor').astype(jnp.float32)  43.8 us
    dot_general x8, matrix products, masked_scores(): jnp.einsum('qhd,khd->hqk', query_rows, key_rows, preferred_element_type=j...  35.2 us
    all_gather x1, waiting for transfers between devices, body(): lax.all_gather(k_rot.reshape(rows_here, local_width), 'dp', axis=0, tiled...  34.1 us
    all_gather x1, blocking collectives, body(): lax.all_gather(keep_here, 'dp', axis=0, tiled=True)  27.1 us
  transfers between devices with their start and end apart: 9, of which 6 were waited for; matrix products, arithmetic and copies ran while one was open for 16% of the time, Pallas kernels for 0%

commit v1 on v0

--- a/solution.py
+++ b/solution.py
@@ -1,7 +1,13 @@
+import functools
+
 import jax
 import jax.numpy as jnp
 from jax import lax
+from jax.experimental import pallas as pl
+from jax.experimental.pallas import tpu as pltpu
 from jax.sharding import PartitionSpec as P
+
+MESH = pl.DeviceIdType.MESH
 
 HDIM = 128
 WIN = 2
@@ -12,6 +18,135 @@
 EPSILON = 1e-05
 ROPE_BASE = 10000.0
 NEGATIVE = -1e30
+
+
+def ring_place(index, count):
+    if count != 8:
+        return index
+    z, y = index // 2, index % 2
+    return z + y * (7 - 2 * z)
+
+
+def ring_index(place, count):
+    place = lax.rem(place + 2 * count, count)
+    if count != 8:
+        return place
+    y = place // 4
+    z = place - y * (2 * place - 7)
+    return z * 2 + y
+
+
+def ring_kernel(count, parts, *refs):
+    ins, outs, slots = refs[:parts], refs[parts : 2 * parts], refs[2 * parts : 3 * parts]
+    send_sem, recv_sem = refs[3 * parts :]
+    me = ring_place(lax.axis_index("dp"), count)
+    tensor = lax.axis_index("tensor")
+    ahead = (
+        (ring_index(me + 1, count), tensor),
+        (ring_index(me - 1, count), tensor),
+    )
+    barrier = pltpu.get_barrier_semaphore()
+    for device in ahead:
+        pl.semaphore_signal(barrier, inc=1, device_id=device, device_id_type=MESH)
+    pl.semaphore_wait(barrier, 2)
+
+    def block(part, way, number):
+        rows = ins[part].shape[1] // count
+        half = ins[part].shape[2] // 2
+        number = lax.rem(number + 2 * count, count)
+        start = pl.multiple_of(number * rows, rows)
+        return (slice(None), pl.ds(start, rows), pl.ds(way * half, half))
+
+    def scatter_copy(part, way, step, source):
+        return pltpu.make_async_remote_copy(
+            src_ref=source,
+            dst_ref=slots[part].at[way, step],
+            send_sem=send_sem.at[0, way, step, part],
+            recv_sem=recv_sem.at[0, way, step, part],
+            device_id=ahead[way],
+            device_id_type=MESH,
+        )
+
+    def gather_copy(part, way, step, number):
+        where = outs[part].at[block(part, way, number)]
+        return pltpu.make_async_remote_copy(
+            src_ref=where,
+            dst_ref=where,
+            send_sem=send_sem.at[1, way, step, part],
+            recv_sem=recv_sem.at[1, way, step, part],
+            device_id=ahead[way],
+            device_id_type=MESH,
+        )
+
+    both = [(part, way) for part in range(parts) for way in (0, 1)]
+    sign = (1, -1)
+    for part, way in both:
+        scatter_copy(part, way, 0, ins[part].at[block(part, way, me)]).start()
+
+    def add_own(part, way, step, target):
+        where = block(part, way, me - sign[way] * (step + 1))
+        depth, rows = ins[part].shape[0], ins[part].shape[1] // count
+        piece = min(rows, 32)
+        for layer in range(depth):
+
+            @pl.loop(0, rows // piece)
+            def _(turn):
+                here = pl.ds(pl.multiple_of(turn * piece, piece), piece)
+                mine = ins[part].at[where].at[layer, here, :]
+                came = slots[part].at[way, step, layer, here, :]
+                total = mine[...].astype(jnp.float32) + came[...].astype(jnp.float32)
+                target.at[layer, here, :][...] = total.astype(jnp.bfloat16)
+
+    @pl.loop(0, count - 2)
+    def _(step):
+        for part, way in both:
+            source = slots[part].at[way, step]
+            scatter_copy(part, way, step, source).wait_recv()
+            add_own(part, way, step, source)
+            scatter_copy(part, way, step + 1, source).start()
+
+    last = count - 2
+    for part, way in both:
+        scatter_copy(part, way, last, slots[part].at[way, last]).wait_recv()
+        mine = me + sign[way]
+        add_own(part, way, last, outs[part].at[block(part, way, mine)])
+        gather_copy(part, way, 0, mine).start()
+
+    @pl.loop(0, count - 2)
+    def _(step):
+        for part, way in both:
+            number = me - sign[way] * step
+            gather_copy(part, way, step, number).wait_recv()
+            gather_copy(part, way, step + 1, number).start()
+
+    for part, way in both:
+        gather_copy(part, way, last, me - sign[way] * last).wait_recv()
+
+    @pl.loop(0, count - 1)
+    def _(step):
+        for part, way in both:
+            scatter_copy(part, way, step, slots[part].at[way, step]).wait_send()
+            gather_copy(part, way, step, me + sign[way] * (1 - step)).wait_send()
+
+
+def ring_sum(arrays, count, number):
+    parts = len(arrays)
+    slots = [
+        pltpu.VMEM((2, count - 1, a.shape[0], a.shape[1] // count, a.shape[2] // 2), jnp.bfloat16)
+        for a in arrays
+    ]
+    sems = pltpu.SemaphoreType.DMA((2, 2, count - 1, parts))
+    return pl.pallas_call(
+        functools.partial(ring_kernel, count, parts),
+        out_shape=[jax.ShapeDtypeStruct(a.shape, jnp.bfloat16) for a in arrays],
+        in_specs=[pl.BlockSpec(memory_space=pltpu.VMEM)] * parts,
+        out_specs=[pl.BlockSpec(memory_space=pltpu.VMEM)] * parts,
+        scratch_shapes=[*slots, sems, sems],
+        compiler_params=pltpu.CompilerParams(
+            collective_id=number, has_side_effects=True, vmem_limit_bytes=60 << 20
+        ),
+        name="ring_sum",
+    )(*arrays)
 
 
 def row_scale(values):
@@ -405,25 +540,40 @@
     input_grad = (
         lax.dynamic_slice_in_dim(hidden_grad, feature_start, local_width, 1) + input_sum
     ).astype(jnp.bfloat16)
-    (
-        attn_gain_grad,
-        qkv_grad,
-        qk_gain_grad,
-        out_grad,
-        ffn_gain_grad,
-        router_grad,
-        expert_in_grad,
-        expert_out_grad,
-    ) = (
-        lax.psum(attn_gain_grad.astype(jnp.bfloat16), "dp").astype(jnp.float32),
-        lax.psum(qkv_grad.astype(jnp.bfloat16), "dp").astype(jnp.float32),
-        lax.psum(qk_gain_grad.astype(jnp.bfloat16), "dp").astype(jnp.float32),
-        lax.psum(out_grad.astype(jnp.bfloat16), "dp").astype(jnp.float32),
-        lax.psum(ffn_gain_grad.astype(jnp.bfloat16), "dp").astype(jnp.float32),
-        lax.psum(router_grad.astype(jnp.bfloat16), "dp").astype(jnp.float32),
-        lax.psum(expert_in_grad.astype(jnp.bfloat16), "dp").astype(jnp.float32),
-        lax.psum(expert_out_grad.astype(jnp.bfloat16), "dp").astype(jnp.float32),
-    )
+    dp_count = lax.axis_size("dp")
+    small = jnp.concatenate(
+        [
+            router_grad.reshape(-1, 256),
+            jnp.concatenate([attn_gain_grad, ffn_gain_grad, qk_gain_grad.reshape(-1)]).reshape(
+                -1, 256
+            ),
+        ]
+    ).astype(jnp.bfloat16)
+    small_rows = small.shape[0]
+    small = jnp.pad(small, ((0, -small_rows % (dp_count * 8)), (0, 0)))
+    low = jnp.bfloat16
+    qkv_sum, out_sum, in_sum, exp_sum, small_sum = ring_sum(
+        [
+            jnp.transpose(qkv_grad, (1, 0, 2)).astype(low),
+            out_grad.astype(low)[None],
+            expert_in_grad.reshape(WIN, model_width, 2 * local_ff).astype(low),
+            expert_out_grad.astype(low),
+            small[None],
+        ],
+        dp_count,
+        0,
+    )
+    qkv_grad = jnp.transpose(qkv_sum.astype(jnp.float32), (1, 0, 2))
+    out_grad = out_sum[0].astype(jnp.float32)
+    expert_in_grad = in_sum.astype(jnp.float32).reshape(expert_in_grad.shape)
+    expert_out_grad = exp_sum.astype(jnp.float32)
+    router_rows = router_grad.size // 256
+    small_sum = small_sum[0].astype(jnp.float32)
+    router_grad = small_sum[:router_rows].reshape(router_grad.shape)
+    gains = small_sum[router_rows:small_rows].reshape(-1)
+    attn_gain_grad = gains[:local_width]
+    ffn_gain_grad = gains[local_width : 2 * local_width]
+    qk_gain_grad = gains[2 * local_width :].reshape(2, local_width)
     return (
         output,
         input_grad,

time: 1290 us -> 1110 us (0.86)
  waiting for transfers between devices: 741 us -> 288 us
  Pallas kernels: 0 us -> 293 us
  blocking collectives: 74.8 us -> 54.4 us
  local copies, waits for them, and re-layouts: 149 us -> 136 us
    psum x1 -> x0, waiting for transfers between devices: 446 us -> none  [body(): lax.psum(expert_in_grad.astype(jnp.bfloat16), 'dp').astype(jnp.float32)]
    pallas_call x0 -> x1, Pallas kernels: none -> 293 us  [ring_sum(): pl.pallas_call(functools.partial(ring_kernel, count, parts), out_shape=[j...]
    unnamed x233, local copies, waits for them, and re-layouts: 69.4 us -> 42.3 us
    psum x1 -> x0, blocking collectives: 19.5 us -> none  [body(): lax.psum(attn_gain_grad.astype(jnp.bfloat16), 'dp').astype(jnp.float32)]
  transfers between devices with their start and end apart: 9 -> 8, of which waited for: 6 -> 5; matrix products, arithmetic and copies ran while one was open for 16% -> 22% of each run, Pallas kernels for 0% -> 27%
where the time goes in v1:
time: 1110 us; the launch traced here: 1100 us
  Pallas kernels  293 us (26%)
  waiting for transfers between devices  288 us (26%)
  matrix products  180 us (16%)
  local copies, waits for them, and re-layouts  136 us (12%)
  other arithmetic  128 us (12%)
  blocking collectives  54.4 us (5%)
  between operations  16.8 us (2%)
    pallas_call x1, Pallas kernels, ring_sum(): pl.pallas_call(functools.partial(ring_kernel, count, parts), out_shape=[j...  293 us
    reduce_scatter x1, waiting for transfers between devices, body(): lax.psum_scatter(kv_terms.reshape(total_rows, 2 * local_width).astype(jnp...  124 us
    all_gather x1, waiting for transfers between devices, body(): lax.all_gather(v_low, 'dp', axis=0, tiled=True)  63.7 us
    psum x1, waiting for transfers between devices, body(): lax.psum(mixture_grad.astype(jnp.bfloat16), 'tensor').astype(jnp.float32)  43.8 us
    unnamed x233, local copies, waits for them, and re-layouts  42.3 us
    dot_general x8, matrix products, masked_scores(): jnp.einsum('qhd,khd->hqk', query_rows, key_rows, preferred_element_type=j...  35.2 us
    all_gather x1, waiting for transfers between devices, body(): lax.all_gather(k_rot.reshape(rows_here, local_width), 'dp', axis=0, tiled...  34 us
    all_gather x1, blocking collectives, body(): lax.all_gather(keep_here, 'dp', axis=0, tiled=True)  27.2 us
  transfers between devices with their start and end apart: 8, of which 5 were waited for; matrix products, arithmetic and copies ran while one was open for 22% of the time, Pallas kernels for 27%

profile of v1, /device:TPU:0, one launch (start us, length us, event | category | flops | bytes accessed | tf_op | source)
XLA Modules:
  0.0 1097.2 jit_solution(1175703319747970824)
XLA Ops:
  7.3 8.9 copy.121
  18.8 6.4 fusion.48
  28.0 8.4 all-reduce.8
  46.3 6.2 fusion.181
  52.5 27.2 %all-gather.1 = bf16[8,1,512]{2,1,0:T(2,128)(2,1)S(1)} all-gather(bf16[1,1,512]{2,1,0:T(2,128)(2,1)S(1)} %reshape.919), channel_id=1, replica_groups=mesh['dp'=8,'tensor'=4] {'dp'}, dimensions={0}, use_global_device_ids=true | all-gather | bytes 9216 | tf_op jit(solution)/shard_map/all_gather | solution.py:290
  80.9 34.0 %all-gather.6.cloned.1.call-done = bf16[4096,512]{1,0:T(8,128)(2,1)} async-done(((bf16[512,512]{1,0:T(8,128)(2,1)}), bf16[4096,512]{1,0:T(8,128)(2,1)}) %all-gather.6.cloned.1.call-update) | async-done | bytes 4194320 | tf_op jit(solution)/shard_map/all_gather | solution.py:288
  114.9 6.9 reshape.788
  121.7 5.2 copy.123
  127.0 63.7 %all-gather.10.cloned.1.call-done = bf16[4096,1,512]{0,2,1:T(8,128)(2,1)} async-done(((bf16[512,1,512]{0,2,1:T(8,128)(2,1)}), bf16[4096,1,512]{0,2,1:T(8,128)(2,1)}) %all-gather.10.cloned.1.call-update) | async-done | bytes 4194320 | tf_op jit(solution)/shard_map/all_gather | solution.py:289
  190.7 7.9 reshape.789
  198.5 5.6 copy.125
  204.1 73.0 %while.28 = (s32[]{:T(128)}, f32[4,512]{1,0:T(4,128)S(1)}, f32[4,512]{1,0:T(4,128)S(1)}, f32[512,4,128]{0,2,1:T(8,128)}, s32[512]{0:T(512)S(1)}, /*index=5*/s32[...) while((s32[]{:T(128)}, f32[4,512]{1,0:T(4,128)S(1)}, ...), condition=%wide.region_15.16_spmd.clone, body=%wide.region_12.15_spmd.clone.sunk | while | flops 1099709440 | bytes 65700036 | solution.py:324
  205.1 6.3 fusion.244
  211.5 4.5 fusion.246
  217.3 4.8 fusion.248
  223.2 6.3 fusion.244
  229.5 4.5 fusion.246
  235.4 5.1 fusion.248
  241.5 6.3 fusion.244
  247.9 4.5 fusion.246
  253.7 5.1 fusion.248
  259.8 6.3 fusion.244
  266.2 4.5 fusion.246
  272.0 5.1 fusion.248
  281.6 3.4 copy.148
  284.9 4.0 copy.126
  288.9 3.4 copy.149
  292.3 4.0 copy.127
  296.6 4.2 convert_element_type.242
  300.8 4.6 gather_fusion.4
  305.4 4.6 gather_fusion.5
  310.0 21.2 %all-reduce.12.cloned.1.call-done = bf16[512,2048]{1,0:T(8,128)(2,1)} async-done(((bf16[512,2048]{1,0:T(8,128)(2,1)}), bf16[512,2048]{1,0:T(8,128)(2,1)}) %all-reduce.12.cloned.1.call-update) | async-done | bytes 2097168 | tf_op jit(solution)/shard_map/psum | solution.py:329
  340.6 4.3 gather_fusion.3
  359.5 6.3 psum.53
  375.8 3.5 fusion.192
  379.2 5.1 scatter_custom_fusion.2
  386.5 3.4 fusion.193
  389.9 7.0 scatter_fusion
  396.9 3.8 convert_element_type.249
  401.0 7.9 copy.131
  409.0 43.8 %all-reduce.14.cloned.1.call-done = bf16[512,2048]{1,0:T(8,128)(2,1)} async-done(((bf16[512,2048]{1,0:T(8,128)(2,1)}), bf16[512,2048]{1,0:T(8,128)(2,1)}) %all-reduce.14.cloned.1.call-update) | async-done | bytes 2097168 | tf_op jit(solution)/shard_map/psum | solution.py:412
  452.9 5.4 multiply_reduce_fusion
  463.7 87.2 %while.29 = (s32[]{:T(128)}, f32[512,4,128]{0,2,1:T(8,128)}, bf16[4,1024,1024]{1,2,0:T(8,128)(2,1)}, bf16[4,1024,4,128]{3,1,2,0:T(8,128)(2,1)}, s32[512]{0:T(512...) while((s32[]{:T(128)}, f32[512,4,128]{0,2,1:T(8,128)}, ...), condition=%wide.region_44.48_spmd.clone, body=%wide.region_43.47_spmd.clone.sunk | while | flops 2714242048 | bytes 145285456 | solution.py:482
  468.0 6.5 fusion.260
  474.5 3.7 fusion.261
  489.8 6.5 fusion.260
  496.3 3.7 fusion.261
  511.5 6.5 fusion.260
  518.0 3.7 fusion.261
  533.3 6.5 fusion.260
  539.7 3.7 fusion.261
  550.9 8.2 copy.147
  560.4 4.6 scatter_custom_fusion
  565.0 7.1 scatter_custom_fusion.1
  572.1 4.0 convert_element_type.239
  582.9 124.4 %reduce-scatter.6.cloned.1.call-done = bf16[512,1024]{0,1:T(8,128)(2,1)} async-done(((bf16[4096,1024]{0,1:T(8,128)(2,1)}), bf16[512,1024]{0,1:T(8,128)(2,1)}) %reduce-scatter.6.cloned.1.call-update) | async-done | bytes 1048592 | tf_op jit(solution)/shard_map/reduce_scatter | solution.py:487
  712.6 6.6 all-reduce.7
  721.6 7.9 fusion.58
  749.9 5.9 all-reduce.6
  756.6 7.1 convert_bitcast_fusion.2.refs_0_
  763.7 292.8 %ring_sum.1 = (bf16[3,2048,512]{2,1,0:T(8,128)(2,1)}, bf16[1,512,2048]{2,1,0:T(8,128)(2,1)}, bf16[2,2048,512]{2,1,0:T(8,128)(2,1)}, bf16[2,256,2048]{2,1,0:T(8,128)(2,1)}, bf16[1,192,256]{2,1,0:T(8,128)(2,1)}) custom-call(bf16[3,2048,512]{2,1,0:T(8,128)(2,1)} %convert_bitcast_fusion.2.refs_0_, bf16[1,512,2048]{2,1,0:T(8,128)(2,1)} %fusion.61.refs_1_, ...), custom_call_target="tpu_custom_call" | custom-call | tf_op jit(solution)/shard_map/ring_sum/pallas_call | solution.py:139
  1061.6 9.6 reshape.814
  1071.2 4.3 convert_element_type.274
  1078.0 9.5 convert_bitcast_fusion
  (476 shorter events, 163.6 us)
Async XLA Ops:
  7.2 271.4 %copy-start = (bf16[512,2048]{1,0:T(8,128)(2,1)S(1)}, bf16[512,2048]{1,0:T(8,128)(2,1)}, u32[]{:S(2)}) copy-start(bf16[512,2048]{1,0:T(8,128)(2,1)} %param.32) | copy-start | bytes 6291460
  7.2 107.7 %all-gather.6.cloned.1.call-start = ((), (), s32[]{:S(2)}) async-start(), calls=%async_computation.3 | async-start | bytes 4718592 | tf_op jit(solution)/shard_map/all_gather | solution.py:288
  7.2 11.6 %copy-start.80 = (f32[2048]{0:T(1024)S(1)}, f32[2048]{0:T(1024)}, u32[]{:S(2)}) copy-start(f32[2048]{0:T(1024)} %param.29) | copy-start | bytes 24580
  27.2 13.0 %copy-start.19 = (f32[512,1,512]{0,2,1:T(8,128)}, f32[512,1,512]{0,2,1:T(8,128)S(1)}, u32[]{:S(2)}) copy-start(f32[512,1,512]{0,2,1:T(8,128)S(1)} %get-tuple-element.514) | copy-start | bytes 3145732
  27.9 12.3 %copy-start.67 = (f32[1,512]{1,0:T(1,128)}, f32[1,512]{1,0:T(1,128)S(1)}, u32[]{:S(2)}) copy-start(f32[1,512]{1,0:T(1,128)S(1)} %get-tuple-element.543) | copy-start | bytes 6148
  28.0 12.3 %copy-start.69 = (f32[1,512]{1,0:T(1,128)}, f32[1,512]{1,0:T(1,128)S(1)}, u32[]{:S(2)}) copy-start(f32[1,512]{1,0:T(1,128)S(1)} %get-tuple-element.544) | copy-start | bytes 6148
  41.3 149.3 %all-gather.10.cloned.1.call-start = ((), (), s32[]{:S(2)}) async-start(), calls=%async_computation.10 | async-start | bytes 4718592 | tf_op jit(solution)/shard_map/all_gather | solution.py:289
  43.5 253.1 %all-gather.8.cloned.1.call-start = ((), (), s32[]{:S(2)}) async-start(), calls=%async_computation.6 | async-start | bytes 2621440 | tf_op jit(solution)/shard_map/all_gather | solution.py:370
  44.2 287.0 %all-reduce.12.cloned.1.call-start = ((), (), s32[]{:S(2)}) async-start(), calls=%async_computation.4 | async-start | bytes 4194304 | tf_op jit(solution)/shard_map/psum | solution.py:329
  44.8 321.0 %copy-start.62 = (pred[512,2]{0,1:T(4,128)(4,1)}, pred[512,2]{0,1:T(4,128)(4,1)S(1)}, u32[]{:S(2)}) copy-start(pred[512,2]{0,1:T(4,128)(4,1)S(1)} %fusion.143) | copy-start | bytes 3076
  46.2 250.3 %copy-start.104 = (s32[128]{0:T(128)}, s32[128]{0:T(128)S(1)}, u32[]{:S(2)}) copy-start(s32[128]{0:T(128)S(1)} %get-tuple-element.566) | copy-start | bytes 1540
  46.2 250.3 %copy-start.102 = (s32[128]{0:T(128)}, s32[128]{0:T(128)S(1)}, u32[]{:S(2)}) copy-start(s32[128]{0:T(128)S(1)} %get-tuple-element.565) | copy-start | bytes 1540
  46.3 291.0 %copy-start.91 = (s32[1024]{0:T(1024)}, s32[1024]{0:T(1024)S(1)}, u32[]{:S(2)}) copy-start(s32[1024]{0:T(1024)S(1)} %pad_clamp_fusion.1) | copy-start | bytes 12292
  46.3 33.5 %copy-start.44 = (bf16[512,4,64]{0,2,1:T(8,128)(2,1)S(1)}, bf16[512,4,64]{0,2,1:T(8,128)(2,1)}, u32[]{:S(2)}) copy-start(bf16[512,4,64]{0,2,1:T(8,128)(2,1)} %get-tuple-element.520) | copy-start | bytes 786436
  281.2 171.5 %all-reduce.14.cloned.1.call-start = ((), (), s32[]{:S(2)}) async-start(), calls=%async_computation.7 | async-start | bytes 4194304 | tf_op jit(solution)/shard_map/psum | solution.py:412
  281.6 59.0 %copy-start.92 = (s32[1024]{0:T(1024)}, s32[1024]{0:T(1024)S(1)}, u32[]{:S(2)}) copy-start(s32[1024]{0:T(1024)S(1)} %pad_clamp_fusion) | copy-start | bytes 12292
  296.5 54.7 %copy-start.106 = (pred[128]{0:T(512)(128)(4,1)}, pred[128]{0:T(512)(128)(4,1)S(1)}, u32[]{:S(2)}) copy-start(pred[128]{0:T(512)(128)(4,1)S(1)} %get-tuple-element.568) | copy-start | bytes 388
  296.5 61.5 %copy-start.108 = (pred[128]{0:T(512)(128)(4,1)}, pred[128]{0:T(512)(128)(4,1)S(1)}, u32[]{:S(2)}) copy-start(pred[128]{0:T(512)(128)(4,1)S(1)} %get-tuple-element.567) | copy-start | bytes 388
  296.5 61.5 %copy-start.112 = (s32[128]{0:T(128)}, s32[128]{0:T(128)S(1)}, u32[]{:S(2)}) copy-start(s32[128]{0:T(128)S(1)} %fusion.164) | copy-start | bytes 1540
  296.5 58.5 %copy-start.87 = (pred[128]{0:T(512)(128)(4,1)}, pred[128]{0:T(512)(128)(4,1)S(1)}, u32[]{:S(2)}) copy-start(pred[128]{0:T(512)(128)(4,1)S(1)} %compare_and_fusion.1) | copy-start | bytes 388
  296.6 54.6 %copy-start.109 = (s32[128]{0:T(128)}, s32[128]{0:T(128)S(1)}, u32[]{:S(2)}) copy-start(s32[128]{0:T(128)S(1)} %fusion.165) | copy-start | bytes 1540
  296.6 50.9 %copy-start.89 = (pred[128]{0:T(512)(128)(4,1)}, pred[128]{0:T(512)(128)(4,1)S(1)}, u32[]{:S(2)}) copy-start(pred[128]{0:T(512)(128)(4,1)S(1)} %compare_and_fusion) | copy-start | bytes 388
  310.0 24.9 %copy-start.65 = (f32[2048]{0:T(1024)S(1)}, f32[2048]{0:T(1024)}, u32[]{:S(2)}) copy-start(f32[2048]{0:T(1024)} %param.33) | copy-start | bytes 24580
  340.6 12.0 %copy-start.27 = (bf16[128,2048]{1,0:T(8,128)(2,1)}, bf16[128,2048]{1,0:T(8,128)(2,1)S(1)}, u32[]{:S(2)}) copy-start(bf16[128,2048]{1,0:T(8,128)(2,1)S(1)} %gather_fusion.1) | copy-start | bytes 1572868
  355.0 20.6 %copy-start.39 = (f32[128,2,256]{2,0,1:T(8,128)}, f32[128,2,256]{2,0,1:T(8,128)S(1)}, u32[]{:S(2)}) copy-start(f32[128,2,256]{2,0,1:T(8,128)S(1)} %fusion.106) | copy-start | bytes 786436
  355.0 15.9 %copy-start.105 = (s32[128]{0:T(128)S(1)}, s32[128]{0:T(128)}, u32[]{:S(2)}) copy-start(s32[128]{0:T(128)} %copy-done.104) | copy-start | bytes 1540
  355.0 18.0 %copy-start.103 = (s32[128]{0:T(128)S(1)}, s32[128]{0:T(128)}, u32[]{:S(2)}) copy-start(s32[128]{0:T(128)} %copy-done.102) | copy-start | bytes 1540
  355.1 18.0 %copy-start.107 = (pred[128]{0:T(512)(128)(4,1)S(1)}, pred[128]{0:T(512)(128)(4,1)}, u32[]{:S(2)}) copy-start(pred[128]{0:T(512)(128)(4,1)} %copy-done.106) | copy-start | bytes 388
  375.6 8.7 copy-start.42
  375.6 8.7 copy-start.90
  375.6 8.7 copy-start.95
  375.8 10.6 copy-start.33
  400.7 306.5 %reduce-scatter.6.cloned.1.call-start = ((), (), s32[]{:S(2)}) async-start(), calls=%async_computation.8 | async-start | bytes 9437184 | tf_op jit(solution)/shard_map/reduce_scatter | solution.py:487
  401.0 51.8 %copy-start.57 = (bf16[2048,64]{0,1:T(8,128)(2,1)S(1)}, bf16[2048,64]{0,1:T(8,128)(2,1)}, u32[]{:S(2)}) copy-start(bf16[2048,64]{0,1:T(8,128)(2,1)} %param.34) | copy-start | bytes 786436
  401.0 51.8 %copy-start.64 = (f32[512,2]{0,1:T(2,128)S(1)}, f32[512,2]{0,1:T(2,128)}, u32[]{:S(2)}) copy-start(f32[512,2]{0,1:T(2,128)} %copy-done.63) | copy-start | bytes 12292
  401.0 51.8 %copy-start.66 = (f32[2048]{0:T(1024)S(1)}, f32[2048]{0:T(1024)}, u32[]{:S(2)}) copy-start(f32[2048]{0:T(1024)} %param.33) | copy-start | bytes 24580
  401.0 51.8 %copy-start.76 = (f32[512]{0:T(512)S(1)}, f32[512]{0:T(512)}, u32[]{:S(2)}) copy-start(f32[512]{0:T(512)} %copy-done.75) | copy-start | bytes 6148
  401.0 51.8 %copy-start.82 = (f32[512]{0:T(512)S(1)}, f32[512]{0:T(512)}, u32[]{:S(2)}) copy-start(f32[512]{0:T(512)} %get-tuple-element.497) | copy-start | bytes 6148
  466.2 8.3 copy-start.4
  468.0 6.5 copy-start.6
  487.9 8.3 copy-start.4
  489.8 6.5 copy-start.6
  509.7 8.3 copy-start.4
  531.4 8.3 copy-start.4
  559.2 188.2 %reduce-scatter.4.cloned.1.call-start = ((), (), s32[]{:S(2)}) async-start(), calls=%async_computation.5 | async-start | bytes 2621440 | tf_op jit(solution)/shard_map/reduce_scatter | solution.py:365
  572.1 7.5 copy-start.17
  572.1 7.5 copy-start.43
  576.1 511.4 %reduce-scatter.8.cloned.1.call-start = ((), (), s32[]{:S(2)}) async-start(), calls=%async_computation.9 | async-start | bytes 2621440 | tf_op jit(solution)/shard_map/reduce_scatter | solution.py:533
  577.4 132.2 %copy-start.8 = (f32[512,4,128]{0,2,1:T(8,128)S(1)}, f32[512,4,128]{0,2,1:T(8,128)}, u32[]{:S(2)}) copy-start(f32[512,4,128]{0,2,1:T(8,128)} %get-tuple-element.158) | copy-start | bytes 3145732
  577.4 132.2 %copy-start.36 = (f32[512,64]{0,1:T(8,128)S(1)}, f32[512,64]{0,1:T(8,128)}, u32[]{:S(2)}) copy-start(f32[512,64]{0,1:T(8,128)} %copy-done.35) | copy-start | bytes 393220
  577.4 132.2 %copy-start.38 = (f32[512,64]{0,1:T(8,128)S(1)}, f32[512,64]{0,1:T(8,128)}, u32[]{:S(2)}) copy-start(f32[512,64]{0,1:T(8,128)} %copy-done.37) | copy-start | bytes 393220
  582.9 127.0 %copy-start.72 = (f32[512]{0:T(512)S(1)}, f32[512]{0:T(512)}, u32[]{:S(2)}) copy-start(f32[512]{0:T(512)} %copy-done.71) | copy-start | bytes 6148
  710.8 8.4 copy-start.78
  710.8 8.4 copy-start.79
  711.9 9.6 copy-start.11
  711.9 9.7 copy-start.81
  711.9 9.7 copy-start.84
  721.5 8.0 copy-start.47
  721.5 7.9 copy-start.49
  721.6 7.9 copy-start.85
  744.7 11.2 %copy-start.56 = (bf16[128,256]{1,0:T(8,128)(2,1)S(1)}, bf16[128,256]{1,0:T(8,128)(2,1)}, u32[]{:S(2)}) copy-start(bf16[128,256]{1,0:T(8,128)(2,1)} %reshape.800) | copy-start | bytes 196612
  744.7 11.9 %copy-start.48 = (bf16[512,1,512]{0,2,1:T(8,128)(2,1)S(1)}, bf16[512,1,512]{0,2,1:T(8,128)(2,1)}, u32[]{:S(2)}) copy-start(bf16[512,1,512]{0,2,1:T(8,128)(2,1)} %copy-done.47) | copy-start | bytes 1572868
  744.7 11.8 %copy-start.50 = (bf16[512,1,512]{0,2,1:T(8,128)(2,1)S(1)}, bf16[512,1,512]{0,2,1:T(8,128)(2,1)}, u32[]{:S(2)}) copy-start(bf16[512,1,512]{0,2,1:T(8,128)(2,1)} %copy-done.49) | copy-start | bytes 1572868
  1078.0 11.9 %copy-start.1 = (bf16[512,2048]{1,0:T(8,128)(2,1)S(1)}, bf16[512,2048]{1,0:T(8,128)(2,1)}, u32[]{:S(2)}) copy-start(bf16[512,2048]{1,0:T(8,128)(2,1)} %param.32) | copy-start | bytes 6291460
  (76 other events, 288.9 us)
Sparse Core Ops, SparseCore 0:
  41.5 73.3 all-gather.5
  117.5 73.1 all-gather.9
  192.2 20.7 all-gather.7
  281.3 49.8 all-reduce.11
  400.9 51.8 all-reduce.13
  559.3 147.9 reduce-scatter.5
  710.4 30.2 reduce-scatter.3
  743.2 31.1 reduce-scatter.7

commit v2 on v1

--- a/solution.py
+++ b/solution.py
@@ -18,6 +18,8 @@
 EPSILON = 1e-05
 ROPE_BASE = 10000.0
 NEGATIVE = -1e30
+LOG2E = 1.4426950408889634
+TILE = 512
 
 
 def ring_place(index, count):
@@ -149,6 +151,467 @@
     )(*arrays)
 
 
+def line_place(count, heads):
+    me = lax.axis_index("dp")
+    across = count // heads
+    return me // across, lax.rem(me, across), across
+
+
+def greet(devices):
+    barrier = pltpu.get_barrier_semaphore()
+    for device in devices:
+        pl.semaphore_signal(barrier, inc=1, device_id=device, device_id_type=MESH)
+    pl.semaphore_wait(barrier, len(devices))
+
+
+def line_devices(count, heads):
+    z, w, across = line_place(count, heads)
+    tensor = lax.axis_index("tensor")
+    along = [(lax.rem(z + dz, heads) * across + w, tensor) for dz in range(1, heads)]
+    beside = [(z * across + lax.rem(w + dw, across), tensor) for dw in range(1, across)]
+    return along, beside
+
+
+def head_columns(number):
+    return (slice(None), pl.ds(pl.multiple_of(number * HDIM, HDIM), HDIM))
+
+
+def spread_kernel(count, heads, q, k, v, keep, q_all, k_all, v_all, keep_all, *sems):
+    send_one, recv_one, send_two, recv_two, near = sems
+    z, w, across = line_place(count, heads)
+    me = z * across + w
+    along, beside = line_devices(count, heads)
+    greet(along + beside)
+    pairs = ((k, k_all), (v, v_all), (keep, keep_all), (q, q_all))
+
+    def piece(item, head):
+        source = pairs[item][0]
+        return source if item == 2 else source.at[head_columns(head)]
+
+    def first_copy(item, dz):
+        head = lax.rem(z + dz, heads)
+        return pltpu.make_async_remote_copy(
+            src_ref=piece(item, head),
+            dst_ref=pairs[item][1].at[z if item == 3 else me],
+            send_sem=send_one.at[item, dz - 1],
+            recv_sem=recv_one.at[item, dz - 1],
+            device_id=along[dz - 1],
+            device_id_type=MESH,
+        )
+
+    def second_copy(item, dz, dw):
+        where = lax.rem(z - dz + heads, heads) * across + w
+        return pltpu.make_async_remote_copy(
+            src_ref=piece(item, z) if dz == 0 else pairs[item][1].at[where],
+            dst_ref=pairs[item][1].at[where],
+            send_sem=send_two.at[item, dz, dw - 1],
+            recv_sem=recv_two.at[item, dz, dw - 1],
+            device_id=beside[dw - 1],
+            device_id_type=MESH,
+        )
+
+    first = [(item, dz) for dz in range(1, heads) for item in range(4)]
+    second = [(dz, item, dw) for dz in range(heads) for item in range(3) for dw in range(1, across)]
+    local = []
+    for item, dz in first:
+        first_copy(item, dz).start()
+    for dz, item, dw in second:
+        if dz == 0:
+            second_copy(item, dz, dw).start()
+    for item in range(4):
+        own = pairs[item][1].at[z if item == 3 else me]
+        copy = pltpu.make_async_copy(piece(item, z), own, near.at[item])
+        copy.start()
+        local.append(copy)
+    for item, dz in first:
+        first_copy(item, dz).wait_recv()
+        if item < 3:
+            for dw in range(1, across):
+                second_copy(item, dz, dw).start()
+    for dz, item, dw in second:
+        second_copy(item, dz, dw).wait_recv()
+    for item, dz in first:
+        first_copy(item, dz).wait_send()
+    for dz, item, dw in second:
+        second_copy(item, dz, dw).wait_send()
+    for copy in local:
+        copy.wait()
+
+
+def spread_heads(q, k, v, keep, count, heads, number):
+    rows = q.shape[0]
+    across = count // heads
+    sem = pltpu.SemaphoreType.DMA
+    shapes = [(heads, rows, HDIM), (count, rows, HDIM), (count, rows, HDIM), (count, *keep.shape)]
+    return pl.pallas_call(
+        functools.partial(spread_kernel, count, heads),
+        out_shape=[jax.ShapeDtypeStruct(shape, jnp.bfloat16) for shape in shapes],
+        in_specs=[pl.BlockSpec(memory_space=pl.ANY)] * 4,
+        out_specs=[pl.BlockSpec(memory_space=pl.ANY)] * 4,
+        scratch_shapes=[
+            sem((4, heads - 1)),
+            sem((4, heads - 1)),
+            sem((3, heads, across - 1)),
+            sem((3, heads, across - 1)),
+            sem((4,)),
+        ],
+        compiler_params=pltpu.CompilerParams(collective_id=number, has_side_effects=True),
+        name="spread_heads",
+    )(q, k, v, keep)
+
+
+def swap_kernel(count, heads, join, source, result, send_sem, recv_sem, near):
+    z, w, across = line_place(count, heads)
+    along, _ = line_devices(count, heads)
+    greet(along)
+
+    def copy_to(dz):
+        far = lax.rem(z + dz, heads)
+        return pltpu.make_async_remote_copy(
+            src_ref=source.at[far] if join else source.at[head_columns(far)],
+            dst_ref=result.at[head_columns(z)] if join else result.at[z],
+            send_sem=send_sem.at[dz - 1],
+            recv_sem=recv_sem.at[dz - 1],
+            device_id=along[dz - 1],
+            device_id_type=MESH,
+        )
+
+    for dz in range(1, heads):
+        copy_to(dz).start()
+    own = pltpu.make_async_copy(
+        source.at[z] if join else source.at[head_columns(z)],
+        result.at[head_columns(z)] if join else result.at[z],
+        near,
+    )
+    own.start()
+    for dz in range(1, heads):
+        copy_to(dz).wait()
+    own.wait()
+
+
+def swap_line(source, count, heads, join, number):
+    rows = source.shape[1] if join else source.shape[0]
+    shape = (rows, heads * HDIM) if join else (heads, rows, HDIM)
+    sem = pltpu.SemaphoreType.DMA
+    return pl.pallas_call(
+        functools.partial(swap_kernel, count, heads, join),
+        out_shape=jax.ShapeDtypeStruct(shape, jnp.bfloat16),
+        in_specs=[pl.BlockSpec(memory_space=pl.ANY)],
+        out_specs=pl.BlockSpec(memory_space=pl.ANY),
+        scratch_shapes=[sem((heads - 1,)), sem((heads - 1,)), sem],
+        compiler_params=pltpu.CompilerParams(collective_id=number, has_side_effects=True),
+        name="join_heads" if join else "part_heads",
+    )(source)
+
+
+def return_kernel(count, heads, dq, dk, dv, dq_own, dk_own, dv_own, came_k, came_v, total_k, total_v, *sems):
+    send_one, recv_one, send_two, recv_two, near = sems
+    z, w, across = line_place(count, heads)
+    along, beside = line_devices(count, heads)
+    greet(along + beside)
+    partial = ((dk, came_k, total_k), (dv, came_v, total_v))
+    whole = (dk_own, dv_own, dq_own)
+    lines = [lax.rem(z + dz, heads) for dz in (*range(1, heads), 0)]
+
+    def first_copy(item, turn, dw):
+        return pltpu.make_async_remote_copy(
+            src_ref=partial[item][0].at[lines[turn] * across + lax.rem(w + dw, across)],
+            dst_ref=partial[item][1].at[turn, dw - 1],
+            send_sem=send_one.at[item, turn, dw - 1],
+            recv_sem=recv_one.at[item, turn, dw - 1],
+            device_id=beside[dw - 1],
+            device_id_type=MESH,
+        )
+
+    def second_copy(item, turn):
+        return pltpu.make_async_remote_copy(
+            src_ref=dq.at[lines[turn]] if item == 2 else partial[item][2].at[turn],
+            dst_ref=whole[item].at[head_columns(z)],
+            send_sem=send_two.at[item, turn],
+            recv_sem=recv_two.at[item, turn],
+            device_id=along[turn],
+            device_id_type=MESH,
+        )
+
+    def landed(item, turn):
+        back = lax.rem(z - turn - 1 + heads, heads)
+        where = whole[item].at[head_columns(back)]
+        return pltpu.make_async_remote_copy(
+            src_ref=where,
+            dst_ref=where,
+            send_sem=send_two.at[item, turn],
+            recv_sem=recv_two.at[item, turn],
+            device_id=along[turn],
+            device_id_type=MESH,
+        )
+
+    rows = dk.shape[1]
+    piece = 128
+    first = [(item, turn, dw) for turn in range(heads) for item in (0, 1) for dw in range(1, across)]
+    for item, turn, dw in first:
+        first_copy(item, turn, dw).start()
+    for turn in range(heads - 1):
+        second_copy(2, turn).start()
+    local = [pltpu.make_async_copy(dq.at[z], dq_own.at[head_columns(z)], near.at[2])]
+    local[0].start()
+    for turn in range(heads):
+        for item in (0, 1):
+            own, came, total = partial[item]
+            for dw in range(1, across):
+                first_copy(item, turn, dw).wait_recv()
+
+            @pl.loop(0, rows // piece)
+            def _(part):
+                here = pl.ds(pl.multiple_of(part * piece, piece), piece)
+                result = own[lines[turn] * across + w, here, :].astype(jnp.float32)
+                for dw in range(1, across):
+                    result = result + came[turn, dw - 1, here, :].astype(jnp.float32)
+                total[turn, here, :] = result.astype(jnp.bfloat16)
+
+            if turn < heads - 1:
+                second_copy(item, turn).start()
+            else:
+                copy = pltpu.make_async_copy(
+                    total.at[turn], whole[item].at[head_columns(z)], near.at[item]
+                )
+                copy.start()
+                local.append(copy)
+    for item in range(3):
+        for turn in range(heads - 1):
+            landed(item, turn).wait_recv()
+            second_copy(item, turn).wait_send()
+    for item, turn, dw in first:
+        first_copy(item, turn, dw).wait_send()
+    for copy in local:
+        copy.wait()
+
+
+def return_heads(dq, dk, dv, count, heads, number):
+    rows = dq.shape[1]
+    across = count // heads
+    sem = pltpu.SemaphoreType.DMA
+    vmem = pl.BlockSpec(memory_space=pltpu.VMEM)
+    came = pltpu.VMEM((heads, across - 1, rows, HDIM), jnp.bfloat16)
+    total = pltpu.VMEM((heads, rows, HDIM), jnp.bfloat16)
+    own = jax.ShapeDtypeStruct((rows, heads * HDIM), jnp.bfloat16)
+    return pl.pallas_call(
+        functools.partial(return_kernel, count, heads),
+        out_shape=[own] * 3,
+        in_specs=[vmem] * 3,
+        out_specs=[vmem] * 3,
+        scratch_shapes=[
+            came,
+            came,
+            total,
+            total,
+            sem((2, heads, across - 1)),
+            sem((2, heads, across - 1)),
+            sem((3, heads - 1)),
+            sem((3, heads - 1)),
+            sem((3,)),
+        ],
+        compiler_params=pltpu.CompilerParams(
+            collective_id=number, has_side_effects=True, vmem_limit_bytes=60 << 20
+        ),
+        name="return_heads",
+    )(dq, dk, dv)
+
+
+def across_rows(left, right):
+    return lax.dot_general(
+        left, right, (((1,), (1,)), ((), ())), preferred_element_type=jnp.float32
+    )
+
+
+def attend_kernel(inverse, first, own, stop, q, k, v, out, out_low, top, k_packed, v_turned):
+    blocks = inverse.shape[0]
+    rate = HDIM**-0.5 * LOG2E
+
+    @pl.loop(0, blocks)
+    def _(b):
+        here = pl.ds(pl.multiple_of(b * BLOCK, BLOCK), BLOCK)
+        there = pl.ds(pl.multiple_of(inverse[b] * BLOCK, BLOCK), BLOCK)
+        k_packed[here, :] = k[there, :]
+        v_turned[:, here] = v[there, :].T
+
+    k_packed[blocks * BLOCK :, :] = jnp.zeros((TILE, HDIM), jnp.bfloat16)
+    v_turned[:, blocks * BLOCK :] = jnp.zeros((HDIM, TILE), jnp.bfloat16)
+    lane = lax.broadcasted_iota(jnp.int32, (1, BLOCK), 1)
+    row = lax.broadcasted_iota(jnp.int32, (TILE, BLOCK), 0)
+
+    @pl.loop(0, own.shape[0])
+    def _(i):
+        rows = pl.ds(pl.multiple_of(i * BLOCK, BLOCK), BLOCK)
+        queries = q[rows, :]
+        start = first[i]
+        limit = jnp.minimum(own[i] * BLOCK + lane, stop[i] - 1)
+        tiles = (own[i] - start) // (TILE // BLOCK) + 1
+
+        def step(t, state):
+            run_top, run_sum, run_out = state
+            base = pl.multiple_of((start * BLOCK) + t * TILE, BLOCK)
+            keys = pl.ds(base, TILE)
+            found = across_rows(k_packed[keys, :], queries)
+            found = jnp.where(row <= limit - base, found, NEGATIVE)
+            new_top = jnp.maximum(run_top, jnp.max(found, axis=0, keepdims=True))
+            factor = jnp.exp2((run_top - new_top) * rate)
+            weights = jnp.exp2((found - new_top) * rate)
+            run_sum = run_sum * factor + jnp.sum(weights, axis=0, keepdims=True)
+            run_out = run_out * factor + jnp.dot(
+                v_turned[:, keys],
+                weights.astype(jnp.bfloat16),
+                preferred_element_type=jnp.float32,
+            )
+            return new_top, run_sum, run_out
+
+        new_top, run_sum, run_out = lax.fori_loop(
+            0,
+            tiles,
+            step,
+            (
+                jnp.full((1, BLOCK), NEGATIVE, jnp.float32),
+                jnp.zeros((1, BLOCK), jnp.float32),
+                jnp.zeros((HDIM, BLOCK), jnp.float32),
+            ),
+        )
+        attended = (run_out / run_sum).T
+        out[rows, :] = attended
+        out_low[rows, :] = attended.astype(jnp.bfloat16)
+        top[i] = jnp.broadcast_to(new_top * rate + jnp.log2(run_sum), (8, BLOCK))
+
+
+def attend_back_kernel(
+    inverse, first, own, stop, q, k, v, out, top, d_out, dq, dk, dv, k_packed, k_turned, v_packed, k_sum, v_sum
+):
+    blocks = inverse.shape[0]
+    scale = HDIM**-0.5
+    rate = scale * LOG2E
+
+    @pl.loop(0, blocks)
+    def _(b):
+        here = pl.ds(pl.multiple_of(b * BLOCK, BLOCK), BLOCK)
+        there = pl.ds(pl.multiple_of(inverse[b] * BLOCK, BLOCK), BLOCK)
+        k_packed[here, :] = k[there, :]
+        k_turned[:, here] = k[there, :].T
+        v_packed[here, :] = v[there, :]
+        k_sum[here, :] = jnp.zeros((BLOCK, HDIM), jnp.float32)
+        v_sum[here, :] = jnp.zeros((BLOCK, HDIM), jnp.float32)
+
+    k_packed[blocks * BLOCK :, :] = jnp.zeros((TILE, HDIM), jnp.bfloat16)
+    k_turned[:, blocks * BLOCK :] = jnp.zeros((HDIM, TILE), jnp.bfloat16)
+    v_packed[blocks * BLOCK :, :] = jnp.zeros((TILE, HDIM), jnp.bfloat16)
+    k_sum[blocks * BLOCK :, :] = jnp.zeros((TILE, HDIM), jnp.float32)
+    v_sum[blocks * BLOCK :, :] = jnp.zeros((TILE, HDIM), jnp.float32)
+    lane = lax.broadcasted_iota(jnp.int32, (1, BLOCK), 1)
+    row = lax.broadcasted_iota(jnp.int32, (TILE, BLOCK), 0)
+
+    @pl.loop(0, own.shape[0])
+    def _(i):
+        rows = pl.ds(pl.multiple_of(i * BLOCK, BLOCK), BLOCK)
+        queries = q[rows, :]
+        incoming = d_out[rows, :]
+        shift = lax.dot_general(
+            jnp.ones((8, HDIM), jnp.float32),
+            incoming.astype(jnp.float32) * out[rows, :],
+            (((1,), (1,)), ((), ())),
+            precision=lax.Precision.HIGHEST,
+            preferred_element_type=jnp.float32,
+        )[0:1]
+        level = top[i][0:1]
+        start = first[i]
+        limit = jnp.minimum(own[i] * BLOCK + lane, stop[i] - 1)
+        tiles = (own[i] - start) // (TILE // BLOCK) + 1
+
+        def step(t, grad):
+            base = pl.multiple_of((start * BLOCK) + t * TILE, BLOCK)
+            keys = pl.ds(base, TILE)
+            found = across_rows(k_packed[keys, :], queries)
+            weights = jnp.where(row <= limit - base, jnp.exp2(found * rate - level), 0.0)
+            dots = across_rows(v_packed[keys, :], incoming)
+            low_grad = (weights * ((dots - shift) * scale)).astype(jnp.bfloat16)
+            v_sum[keys, :] += jnp.dot(
+                weights.astype(jnp.bfloat16), incoming, preferred_element_type=jnp.float32
+            )
+            k_sum[keys, :] += jnp.dot(low_grad, queries, preferred_element_type=jnp.float32)
+            return grad + jnp.dot(
+                k_turned[:, keys], low_grad, preferred_element_type=jnp.float32
+            )
+
+        grad = lax.fori_loop(0, tiles, step, jnp.zeros((HDIM, BLOCK), jnp.float32))
+        dq[rows, :] = grad.T.astype(jnp.bfloat16)
+
+    @pl.loop(0, blocks)
+    def _(b):
+        here = pl.ds(pl.multiple_of(b * BLOCK, BLOCK), BLOCK)
+        there = pl.ds(pl.multiple_of(inverse[b] * BLOCK, BLOCK), BLOCK)
+        dk[there, :] = k_sum[here, :].astype(jnp.bfloat16)
+        dv[there, :] = v_sum[here, :].astype(jnp.bfloat16)
+
+
+def attend_calls(tables, q, k, v):
+    smem = pl.BlockSpec(memory_space=pltpu.SMEM)
+    vmem = pl.BlockSpec(memory_space=pltpu.VMEM)
+    rows, all_rows = q.shape[0], k.shape[0]
+    shape = jax.ShapeDtypeStruct
+    f32, low = jnp.float32, jnp.bfloat16
+    params = pltpu.CompilerParams(vmem_limit_bytes=60 << 20)
+    wide = pltpu.VMEM((HDIM, all_rows + TILE), low)
+    tall = pltpu.VMEM((all_rows + TILE, HDIM), low)
+    tall_sum = pltpu.VMEM((all_rows + TILE, HDIM), f32)
+    out, out_low, top = pl.pallas_call(
+        attend_kernel,
+        out_shape=[
+            shape((rows, HDIM), f32),
+            shape((rows, HDIM), low),
+            shape((rows // BLOCK, 8, BLOCK), f32),
+        ],
+        in_specs=[smem] * 4 + [vmem] * 3,
+        out_specs=[vmem] * 3,
+        scratch_shapes=[tall, wide],
+        compiler_params=params,
+        name="attend",
+    )(*tables, q, k, v)
+
+    def back(d_out):
+        return pl.pallas_call(
+            attend_back_kernel,
+            out_shape=[shape((rows, HDIM), low), shape((all_rows, HDIM), low), shape((all_rows, HDIM), low)],
+            in_specs=[smem] * 4 + [vmem] * 6,
+            out_specs=[vmem] * 3,
+            scratch_shapes=[tall, wide, tall, tall_sum, tall_sum],
+            compiler_params=params,
+            name="attend_back",
+        )(*tables, q, k, v, out, top, d_out)
+
+    return out_low, back
+
+
+def block_tables(seq_blocks, block_place, keep_all, line_rows, heads, count):
+    total = block_place.shape[0]
+    per = total // count
+    seq_ends = jnp.cumsum(seq_blocks)
+    seq_firsts = seq_ends - seq_blocks
+    numbers = jnp.arange(total, dtype=jnp.int32)
+    inverse = jnp.sum(
+        jnp.where(block_place[None, :] == numbers[:, None], numbers[None, :], 0), axis=1
+    )
+    seq_of = jnp.sum((block_place[:, None] >= seq_ends[None, :]).astype(jnp.int32), axis=1)
+    is_seq = seq_of[:, None] == jnp.arange(seq_blocks.shape[0], dtype=jnp.int32)[None, :]
+    kept_blocks = jnp.sum(keep_all.reshape(total, BLOCK).astype(jnp.int32), axis=1)
+    kept = jnp.sum(jnp.where(is_seq, kept_blocks[:, None], 0), axis=0)
+    stop_of = seq_firsts * BLOCK + kept
+    table = jnp.stack(
+        [
+            jnp.sum(jnp.where(is_seq, seq_firsts[None, :], 0), axis=1),
+            block_place,
+            jnp.sum(jnp.where(is_seq, stop_of[None, :], 0), axis=1),
+        ]
+    ).reshape(3, heads, count // heads, per)
+    w = lax.rem(lax.axis_index("dp"), count // heads)
+    mine = lax.dynamic_slice_in_dim(table, w, 1, 2).reshape(3, heads * per)
+    return inverse, mine[0], mine[1], mine[2]
+
+
 def row_scale(values):
     return lax.rsqrt(jnp.mean(values * values, axis=-1, keepdims=True) + EPSILON)
 
@@ -200,42 +663,6 @@
     scaled = gain_row * incoming
     inner_sum = jnp.sum(scaled * values, axis=-1, keepdims=True)
     return row_factor * scaled - values * (row_factor**3 / model_width) * inner_sum
-
-
-def masked_scores(query_rows, seg_rows, pos_rows, key_rows, seg_cols, pos_cols, keep_cols):
-    raw_scores = jnp.einsum(
-        "qhd,khd->hqk", query_rows, key_rows, preferred_element_type=jnp.float32
-    )
-    allowed = (
-        (seg_rows[:, None] == seg_cols[None, :])
-        & (pos_cols[None, :] <= pos_rows[:, None])
-        & (keep_cols[None, :] > 0)
-    )
-    return jnp.where(allowed[None], raw_scores * HDIM ** (-0.5), NEGATIVE)
-
-
-def score_grads(
-    query_rows,
-    seg_rows,
-    pos_rows,
-    top_rows,
-    shift_rows,
-    du_rows,
-    key_rows,
-    value_rows,
-    seg_cols,
-    pos_cols,
-    keep_cols,
-):
-    weights = jnp.exp(
-        masked_scores(query_rows, seg_rows, pos_rows, key_rows, seg_cols, pos_cols, keep_cols)
-        - top_rows[:, :, None]
-    )
-    value_dots = jnp.einsum("qhd,khd->hqk", du_rows, value_rows, preferred_element_type=jnp.float32)
-    score_grad = (weights * (value_dots - shift_rows[:, :, None]) * HDIM ** (-0.5)).astype(
-        jnp.bfloat16
-    )
-    return (weights.astype(jnp.bfloat16), score_grad)
 
 
 def body(
@@ -284,48 +711,29 @@
     k_rot = rotate(k_norm, pos_q).astype(jnp.bfloat16)
     v_low = values_here.astype(jnp.bfloat16)
     keep_here = pad_mask.astype(jnp.bfloat16)
-    k_all, v_all, keep_all = (
-        lax.all_gather(k_rot.reshape(rows_here, local_width), "dp", axis=0, tiled=True),
-        lax.all_gather(v_low, "dp", axis=0, tiled=True),
-        lax.all_gather(keep_here, "dp", axis=0, tiled=True),
-    )
-    total_rows = k_all.shape[0]
-    all_ids = jnp.arange(total_rows, dtype=jnp.int32)
-    seg_keys, pos_keys = token_tables(seq_blocks, block_place, all_ids)
-    key_block = min(1024, total_rows)
-    block_count = total_rows // key_block
-    keys_blocks = k_all.reshape(block_count, key_block, heads_here, HDIM)
-    values_blocks = v_all.reshape(block_count, key_block, heads_here, HDIM)
-    seg_blocks = seg_keys.reshape(block_count, key_block)
-    pos_blocks = pos_keys.reshape(block_count, key_block)
-    keep_blocks = keep_all.reshape(block_count, key_block)
-
-    def online_step(carry_state, block_in):
-        run_top, row_acc, value_acc = carry_state
-        keys_b, values_b, seg_b, pos_b, keep_b = block_in
-        found = masked_scores(q_rot, seg_q, pos_q, keys_b, seg_b, pos_b, keep_b)
-        new_top = jnp.maximum(run_top, jnp.max(found, axis=-1))
-        factor = jnp.exp(run_top - new_top)
-        weights = jnp.exp(found - new_top[:, :, None])
-        row_acc = row_acc * factor + jnp.sum(weights, axis=-1)
-        value_acc = value_acc * jnp.transpose(factor)[:, :, None] + jnp.einsum(
-            "hqk,khd->qhd",
-            weights.astype(jnp.bfloat16),
-            values_b,
-            preferred_element_type=jnp.float32,
-        )
-        return ((new_top, row_acc, value_acc), None)
-
-    start_state = (
-        jnp.full((heads_here, rows_here), NEGATIVE, jnp.float32),
-        jnp.zeros((heads_here, rows_here), jnp.float32),
-        jnp.zeros((rows_here, heads_here, HDIM), jnp.float32),
-    )
-    (row_top, row_sum, value_sum), _ = lax.scan(
-        online_step, start_state, (keys_blocks, values_blocks, seg_blocks, pos_blocks, keep_blocks)
-    )
-    attended = value_sum / jnp.transpose(row_sum)[:, :, None]
-    attended_low = attended.astype(jnp.bfloat16).reshape(rows_here, local_width)
+    dp_count = lax.axis_size("dp")
+    q_line, k_all, v_all, keep_all = spread_heads(
+        q_rot.reshape(rows_here, local_width),
+        k_rot.reshape(rows_here, local_width),
+        v_low,
+        jnp.broadcast_to(keep_here[None], (8, rows_here)),
+        dp_count,
+        heads_here,
+        1,
+    )
+    tables = block_tables(
+        seq_blocks, block_place, keep_all[:, 0], rows_here, heads_here, dp_count
+    )
+    total_rows = dp_count * rows_here
+    line_out, attend_back = attend_calls(
+        tables,
+        q_line.reshape(heads_here * rows_here, HDIM),
+        k_all.reshape(total_rows, HDIM),
+        v_all.reshape(total_rows, HDIM),
+    )
+    attended_low = swap_line(
+        line_out.reshape(heads_here, rows_here, HDIM), dp_count, heads_here, True, 2
+    )
     branch = lax.psum(
         jnp.dot(attended_low, w_out, preferred_element_type=jnp.float32).astype(jnp.bfloat16),
         "tensor",
@@ -436,63 +844,21 @@
     out_grad = jnp.einsum(
         "tc,td->cd", attended_low, branch_grad, preferred_element_type=jnp.float32
     )
-    attended_grad = (
-        jnp.einsum("td,cd->tc", branch_grad, w_out, preferred_element_type=jnp.float32)
-        .astype(jnp.bfloat16)
-        .reshape(rows_here, heads_here, HDIM)
-    )
-    grad_wide = attended_grad.astype(jnp.float32)
-    delta_rows = jnp.transpose(jnp.sum(grad_wide * attended, axis=-1))
-    scaled_grad = (grad_wide / jnp.transpose(row_sum)[:, :, None]).astype(jnp.bfloat16)
-    shift_rows = delta_rows / row_sum
-
-    def key_step(carry_sum, block_in):
-        keys_b, values_b, seg_b, pos_b, keep_b = block_in
-        low_weights, score_grad = score_grads(
-            q_rot,
-            seg_q,
-            pos_q,
-            row_top,
-            shift_rows,
-            scaled_grad,
-            keys_b,
-            values_b,
-            seg_b,
-            pos_b,
-            keep_b,
-        )
-        carry_sum = carry_sum + jnp.einsum(
-            "hqk,khd->qhd", score_grad, keys_b, preferred_element_type=jnp.float32
-        )
-        key_term = jnp.einsum("hqk,qhd->khd", score_grad, q_rot, preferred_element_type=jnp.float32)
-        value_term = jnp.einsum(
-            "hqk,qhd->khd", low_weights, scaled_grad, preferred_element_type=jnp.float32
-        )
-        return (
-            carry_sum,
-            jnp.concatenate(
-                [
-                    key_term.reshape(key_block, local_width),
-                    value_term.reshape(key_block, local_width),
-                ],
-                axis=1,
-            ),
-        )
-
-    query_grad, kv_terms = lax.scan(
-        key_step,
-        jnp.zeros((rows_here, heads_here, HDIM), jnp.float32),
-        (keys_blocks, values_blocks, seg_blocks, pos_blocks, keep_blocks),
-    )
-    kv_grad = lax.psum_scatter(
-        kv_terms.reshape(total_rows, 2 * local_width).astype(jnp.bfloat16),
-        "dp",
-        scatter_dimension=0,
-        tiled=True,
-    ).astype(jnp.float32)
-    key_grad = kv_grad[:, :local_width]
-    value_grad = kv_grad[:, local_width:]
-    value_low_grad = value_grad.astype(jnp.bfloat16)
+    attended_grad = jnp.einsum(
+        "td,cd->tc", branch_grad, w_out, preferred_element_type=jnp.float32
+    ).astype(jnp.bfloat16)
+    line_grad = swap_line(attended_grad, dp_count, heads_here, False, 3)
+    dq_line, dk_line, dv_line = attend_back(line_grad.reshape(heads_here * rows_here, HDIM))
+    query_grad, key_grad, value_low_grad = return_heads(
+        dq_line.reshape(heads_here, rows_here, HDIM),
+        dk_line.reshape(dp_count, rows_here, HDIM),
+        dv_line.reshape(dp_count, rows_here, HDIM),
+        dp_count,
+        heads_here,
+        4,
+    )
+    query_grad = query_grad.astype(jnp.float32).reshape(rows_here, heads_here, HDIM)
+    key_grad = key_grad.astype(jnp.float32)
     _, rope_pull = jax.vjp(lambda turned: rotate(turned, pos_q), q_norm)
     q_norm_grad = rope_pull(query_grad)[0].reshape(rows_here, local_width)
     k_norm_grad = rope_pull(key_grad.reshape(rows_here, heads_here, HDIM))[0].reshape(
@@ -540,7 +906,6 @@
     input_grad = (
         lax.dynamic_slice_in_dim(hidden_grad, feature_start, local_width, 1) + input_sum
     ).astype(jnp.bfloat16)
-    dp_count = lax.axis_size("dp")
     small = jnp.concatenate(
         [
             router_grad.reshape(-1, 256),

time: 1110 us -> 845 us (0.76)
  waiting for transfers between devices: 288 us -> 64.2 us
  Pallas kernels: 293 us -> 451 us
  matrix products: 180 us -> 71.8 us
  local copies, waits for them, and re-layouts: 136 us -> 88 us
  blocking collectives: 54.4 us -> 27.1 us
    pallas_call x0 -> x6, Pallas kernels: none -> 154 us  [the longest x1 42.2 us: return_heads(): pl.pallas_call(functools.partial(return_kernel, count, heads), out_shape=...]
    reduce_scatter x1 -> x0, waiting for transfers between devices: 124 us -> none  [body(): lax.psum_scatter(kv_terms.reshape(total_rows, 2 * local_width).astype(jnp...]
    dot_general x28 -> x0, matrix products: 112 us -> none  [the longest x8 35.2 us: masked_scores(): jnp.einsum('qhd,khd->hqk', query_rows, key_rows, preferred_element_type=j...]
    all_gather x2 -> x0, waiting for transfers between devices: 97.6 us -> none  [the longest x1 63.7 us: body(): lax.all_gather(v_low, 'dp', axis=0, tiled=True)]
    all_gather x1 -> x0, blocking collectives: 27.2 us -> none  [body(): lax.all_gather(keep_here, 'dp', axis=0, tiled=True)]
    psum x1, waiting for transfers between devices: 43.8 us -> 23.9 us  [body(): lax.psum(mixture_grad.astype(jnp.bfloat16), 'tensor').astype(jnp.float32)]
    unnamed x233 -> x154, local copies, waits for them, and re-layouts: 42.3 us -> 22.5 us
    reduce_sum x6, other arithmetic: 18.5 us -> 1.32 us  [the longest x1 0.69 us: block_tables(): jnp.sum(jnp.where(block_place[None, :] == numbers[:, None], numbers[None,...]
  transfers between devices with their start and end apart: 8 -> 5, of which waited for: 5 -> 3; matrix products, arithmetic and copies ran while one was open for 22% -> 20% of each run, Pallas kernels for 27% -> 45%
where the time goes in v2:
time: 845 us; the launch traced here: 836 us
  Pallas kernels  451 us (53%)
  other arithmetic  118 us (14%)
  local copies, waits for them, and re-layouts  88 us (10%)
  matrix products  71.8 us (8%)
  waiting for transfers between devices  64.2 us (8%)
  blocking collectives  27.1 us (3%)
  between operations  15.8 us (2%)
    pallas_call x1, Pallas kernels, ring_sum(): pl.pallas_call(functools.partial(ring_kernel, count, parts), out_shape=[j...  297 us
    pallas_call x1, Pallas kernels, return_heads(): pl.pallas_call(functools.partial(return_kernel, count, heads), out_shape=...  42.2 us
    pallas_call x1, Pallas kernels, spread_heads(): pl.pallas_call(functools.partial(spread_kernel, count, heads), out_shape=...  38.5 us
    psum x1, waiting for transfers between devices, body(): lax.psum(jnp.dot(attended_low, w_out, preferred_element_type=jnp.float32)...  36.2 us
    pallas_call x2, Pallas kernels, swap_line(): pl.pallas_call(functools.partial(swap_kernel, count, heads, join), out_sh...  31.9 us
    psum x1, waiting for transfers between devices, body(): lax.psum(mixture_grad.astype(jnp.bfloat16), 'tensor').astype(jnp.float32)  23.9 us
    pallas_call x1, Pallas kernels, back(): pl.pallas_call(attend_back_kernel, out_shape=[shape((rows, HDIM), low), s...  22.6 us
    unnamed x154, local copies, waits for them, and re-layouts  22.5 us
  transfers between devices with their start and end apart: 5, of which 3 were waited for; matrix products, arithmetic and copies ran while one was open for 20% of the time, Pallas kernels for 45%

profile of v2, /device:TPU:0, one launch (start us, length us, event | category | flops | bytes accessed | tf_op | source)
XLA Modules:
  0.0 836.2 jit_solution(2165070280759727664)
XLA Ops:
  7.3 8.9 %copy.59 = bf16[2048,3,512]{0,2,1:T(8,128)(2,1)} copy(bf16[2048,3,512]{2,0,1:T(8,128)(2,1)} %param.26) | data formatting | bytes 12582912 | tf_op args[6]
  18.8 6.5 fusion
  31.6 2.6 squeeze.54
  34.1 8.4 all-reduce.8
  45.6 2.5 multiply_multiply_fusion.1
  53.7 38.5 %spread_heads.1 = (bf16[4,512,128]{2,1,0:T(8,128)(2,1)}, bf16[8,512,128]{2,1,0:T(8,128)(2,1)}, bf16[8,512,128]{2,1,0:T(8,128)(2,1)}, bf16[8,8,512]{2,1,0:T(8,128)(2,1)}) custom-call(bf16[512,512]{1,0:T(8,128)(2,1)} %bitcast.286, bf16[512,512]{1,0:T(8,128)(2,1)} %bitcast.287, bf16[512,512]{1,0:T(8,128)(2,1)} %fusion.47.v, bf16[8,512]{1,0:T(8,128)(2,1)} %broadcast_in_dim.120.keep), custom_call_target="tpu_custom_call" | custom-call | tf_op jit(solution)/shard_map/spread_heads/pallas_call | solution.py:246
  95.5 18.7 %attend.1 = (f32[2048,128]{1,0:T(8,128)}, bf16[2048,128]{1,0:T(8,128)(2,1)}, f32[16,8,128]{2,1,0:T(8,128)}) custom-call(s32[32]{0:T(128)} %select_reduce_fusion.3.inverse, s32[16]{0:T(128)} %squeeze.58.first, s32[16]{0:T(128)} %squeeze.59.own, s32[16]{0:T(128)} %squeeze.60.stop, bf16[2048,128]{1,0:T(8,128)(2,1)} %bitcast.291, bf16[4096,128]{1,0:T(8,128)(2,1)} %bitcast.282, ...), custom_call_target="tpu_custom_call" | custom-call | tf_op jit(solution)/shard_map/attend/pallas_call | solution.py:561
  114.2 18.9 %join_heads.1 = bf16[512,512]{1,0:T(8,128)(2,1)} custom-call(bf16[4,512,128]{2,1,0:T(8,128)(2,1)} %bitcast.300), custom_call_target="tpu_custom_call" | custom-call | tf_op jit(solution)/shard_map/join_heads/pallas_call | solution.py:296
  133.2 3.6 convolution_convert_fusion.3
  139.9 5.9 fusion.119
  147.6 3.9 copy.63
  151.5 3.4 copy.77
  154.9 3.9 copy.64
  160.0 36.2 %all-reduce.12.cloned.1.call-done = bf16[512,2048]{1,0:T(8,128)(2,1)} async-done(((bf16[512,2048]{1,0:T(8,128)(2,1)}), bf16[512,2048]{1,0:T(8,128)(2,1)}) %all-reduce.12.cloned.1.call-update) | async-done | bytes 2097168 | tf_op jit(solution)/shard_map/psum | solution.py:737
  196.2 3.1 multiply_reduce_fusion.2
  199.9 2.4 multiply_convert_fusion
  202.3 3.4 gather_fusion.1
  205.7 3.5 gather_fusion.3
  209.2 2.6 fusion.123
  212.5 3.2 fusion.50
  217.2 3.2 all-gather.2.cloned.1.call-done
  220.4 4.1 convert_element_type.226
  224.6 3.8 gather_fusion.4
  228.3 4.7 gather_fusion.5
  233.1 3.0 multiply_reduce_fusion.5
  239.2 2.7 multiply_reduce_fusion.6
  246.4 6.6 psum.53
  262.6 3.4 fusion.128
  266.0 5.1 scatter_custom_fusion.2
  275.5 3.5 fusion.129
  279.0 7.0 scatter_fusion
  285.9 3.8 convert_element_type.233
  291.8 5.2 scatter_custom_fusion
  297.0 7.3 scatter_custom_fusion.1
  304.2 3.9 convert_element_type.223
  308.1 3.2 fusion.12
  311.3 2.9 fusion.15
  314.3 2.2 fusion.14
  318.4 23.9 %all-reduce.14.cloned.1.call-done = bf16[512,2048]{1,0:T(8,128)(2,1)} async-done(((bf16[512,2048]{1,0:T(8,128)(2,1)}), bf16[512,2048]{1,0:T(8,128)(2,1)}) %all-reduce.14.cloned.1.call-update) | async-done | bytes 2097168 | tf_op jit(solution)/shard_map/psum | solution.py:820
  342.4 5.5 multiply_reduce_fusion
  348.0 3.2 subtract_add_fusion
  355.3 12.9 %part_heads.1 = bf16[4,512,128]{2,1,0:T(8,128)(2,1)} custom-call(bf16[512,512]{1,0:T(8,128)(2,1)} %convolution_convert_fusion.6.source), custom_call_target="tpu_custom_call" | custom-call | tf_op jit(solution)/shard_map/part_heads/pallas_call | solution.py:296
  368.3 22.6 %attend_back.1 = (bf16[2048,128]{1,0:T(8,128)(2,1)}, bf16[4096,128]{1,0:T(8,128)(2,1)}, bf16[4096,128]{1,0:T(8,128)(2,1)}) custom-call(s32[32]{0:T(128)} %select_reduce_fusion.3.inverse, s32[16]{0:T(128)} %squeeze.58.first, s32[16]{0:T(128)} %squeeze.59.own, s32[16]{0:T(128)} %squeeze.60.stop, bf16[2048,128]{1,0:T(8,128)(2,1)} %bitcast.292, ...), custom_call_target="tpu_custom_call" | custom-call | tf_op jit(solution)/shard_map/attend_back/pallas_call | solution.py:576
  390.9 42.2 %return_heads.1 = (bf16[512,512]{1,0:T(8,128)(2,1)}, bf16[512,512]{1,0:T(8,128)(2,1)}, bf16[512,512]{1,0:T(8,128)(2,1)}) custom-call(bf16[4,512,128]{2,1,0:T(8,128)(2,1)} %bitcast.299, bf16[8,512,128]{2,1,0:T(8,128)(2,1)} %bitcast.297, bf16[8,512,128]{2,1,0:T(8,128)(2,1)} %bitcast.298), custom_call_target="tpu_custom_call" | custom-call | tf_op jit(solution)/shard_map/return_heads/pallas_call | solution.py:397
  435.8 2.3 multiply_add_fusion.3
  441.1 2.7 multiply_reduce_fusion.3
  445.3 2.3 fusion.27
  447.6 6.0 all-reduce.7
  453.6 2.7 subtract_convert_fusion.1
  456.3 6.8 fusion.10
  463.1 2.3 fusion.7
  467.9 3.2 pad_maximum_fusion.1.refs_3_
  471.1 2.4 pad_maximum_fusion.refs_2_
  474.8 2.6 copy.67
  478.2 6.2 all-reduce.6
  485.2 5.3 fusion.13.refs_1_
  490.5 5.8 convert_bitcast_fusion.1.refs_0_
  496.3 297.2 %ring_sum.1 = (bf16[3,2048,512]{2,1,0:T(8,128)(2,1)}, bf16[1,512,2048]{2,1,0:T(8,128)(2,1)}, bf16[2,2048,512]{2,1,0:T(8,128)(2,1)}, bf16[2,256,2048]{2,1,0:T(8,128)(2,1)}, bf16[1,192,256]{2,1,0:T(8,128)(2,1)}) custom-call(bf16[3,2048,512]{2,1,0:T(8,128)(2,1)} %convert_bitcast_fusion.1.refs_0_, bf16[1,512,2048]{2,1,0:T(8,128)(2,1)} %fusion.13.refs_1_, ...), custom_call_target="tpu_custom_call" | custom-call | tf_op jit(solution)/shard_map/ring_sum/pallas_call | solution.py:141
  798.6 9.6 %reshape.674 = f32[2,2048,2,256]{3,2,1,0:T(2,128)} reshape(bf16[2,2048,512]{2,1,0:T(8,128)(2,1)} %get-tuple-element.47) | data formatting | bytes 12582912 | tf_op jit(solution)/shard_map/reshape | solution.py:933
  808.2 4.3 convert_element_type.253
  812.4 2.5 bitcast_convert_fusion
  815.0 9.5 %convert_bitcast_fusion = f32[2048,3,512]{2,0,1:T(8,128)} fusion(bf16[3,2048,512]{2,1,0:T(8,128)(2,1)} %get-tuple-element.45), kind=kLoop, calls=%fused_computation.12 | loop fusion | flops 3145728 | bytes 18874368 | tf_op jit(solution)/shard_map/transpose | solution.py:931
  824.5 2.3 add_convert_fusion.1
  826.9 2.3 add_convert_fusion
  (271 shorter events, 76.1 us)
Async XLA Ops:
  7.2 126.0 %copy-start = (bf16[512,2048]{1,0:T(8,128)(2,1)S(1)}, bf16[512,2048]{1,0:T(8,128)(2,1)}, u32[]{:S(2)}) copy-start(bf16[512,2048]{1,0:T(8,128)(2,1)} %param.28) | copy-start | bytes 6291460
  7.2 189.0 %all-reduce.12.cloned.1.call-start = ((), (), s32[]{:S(2)}) async-start(), calls=%async_computation.2 | async-start | bytes 4194304 | tf_op jit(solution)/shard_map/psum | solution.py:737
  7.2 11.6 %copy-start.49 = (f32[2048]{0:T(1024)S(1)}, f32[2048]{0:T(1024)}, u32[]{:S(2)}) copy-start(f32[2048]{0:T(1024)} %param.25) | copy-start | bytes 24580
  18.8 6.6 copy-start.52
  25.4 3.2 copy-start.65
  25.4 5.5 copy-start.64
  25.4 5.7 copy-start.69
  30.9 18.9 %copy-start.8 = (f32[512,4,128]{2,1,0:T(4,128)}, f32[512,4,128]{2,1,0:T(4,128)S(1)}, u32[]{:S(2)}) copy-start(f32[512,4,128]{2,1,0:T(4,128)S(1)} %squeeze.56) | copy-start | bytes 3145732
  31.0 18.9 %copy-start.34 = (f32[1,512]{1,0:T(1,128)}, f32[1,512]{1,0:T(1,128)S(1)}, u32[]{:S(2)}) copy-start(f32[1,512]{1,0:T(1,128)S(1)} %get-tuple-element.142) | copy-start | bytes 6148
  31.0 18.9 %copy-start.36 = (f32[1,512]{1,0:T(1,128)}, f32[1,512]{1,0:T(1,128)S(1)}, u32[]{:S(2)}) copy-start(f32[1,512]{1,0:T(1,128)S(1)} %get-tuple-element.143) | copy-start | bytes 6148
  43.1 2.5 copy-start.40
  43.1 5.1 copy-start.38
  44.1 5.8 copy-start.20
  49.9 3.2 copy-start.66
  133.2 4.5 copy-start.46
  136.8 83.6 %all-gather.2.cloned.1.call-start = ((), (), s32[]{:S(2)}) async-start(), calls=%async_computation.4 | async-start | bytes 2621440 | tf_op jit(solution)/shard_map/all_gather | solution.py:778
  137.6 204.8 %all-reduce.14.cloned.1.call-start = ((), (), s32[]{:S(2)}) async-start(), calls=%async_computation.5 | async-start | bytes 4194304 | tf_op jit(solution)/shard_map/psum | solution.py:820
  139.1 20.3 %copy-start.68 = (s32[128]{0:T(128)}, s32[128]{0:T(128)S(1)}, u32[]{:S(2)}) copy-start(s32[128]{0:T(128)S(1)} %get-tuple-element.165) | copy-start | bytes 1540
  139.1 20.8 %copy-start.67 = (s32[128]{0:T(128)}, s32[128]{0:T(128)S(1)}, u32[]{:S(2)}) copy-start(s32[128]{0:T(128)S(1)} %get-tuple-element.164) | copy-start | bytes 1540
  139.8 62.5 %copy-start.60 = (s32[1024]{0:T(1024)}, s32[1024]{0:T(1024)S(1)}, u32[]{:S(2)}) copy-start(s32[1024]{0:T(1024)S(1)} %pad_clamp_fusion.1) | copy-start | bytes 12292
  154.9 45.0 %copy-start.32 = (f32[2048]{0:T(1024)S(1)}, f32[2048]{0:T(1024)}, u32[]{:S(2)}) copy-start(f32[2048]{0:T(1024)} %param.29) | copy-start | bytes 24580
  158.8 46.8 %copy-start.61 = (s32[1024]{0:T(1024)}, s32[1024]{0:T(1024)S(1)}, u32[]{:S(2)}) copy-start(s32[1024]{0:T(1024)S(1)} %pad_clamp_fusion) | copy-start | bytes 12292
  159.4 53.1 %copy-start.56 = (pred[128]{0:T(512)(128)(4,1)}, pred[128]{0:T(512)(128)(4,1)S(1)}, u32[]{:S(2)}) copy-start(pred[128]{0:T(512)(128)(4,1)S(1)} %compare_and_fusion.1) | copy-start | bytes 388
  159.9 73.1 %copy-start.58 = (pred[128]{0:T(512)(128)(4,1)}, pred[128]{0:T(512)(128)(4,1)S(1)}, u32[]{:S(2)}) copy-start(pred[128]{0:T(512)(128)(4,1)S(1)} %compare_and_fusion) | copy-start | bytes 388
  196.2 3.7 copy-start.2
  196.2 3.7 copy-start.6
  199.9 5.8 copy-start.42
  205.7 10.0 %copy-start.17 = (bf16[128,2048]{1,0:T(8,128)(2,1)}, bf16[128,2048]{1,0:T(8,128)(2,1)S(1)}, u32[]{:S(2)}) copy-start(bf16[128,2048]{1,0:T(8,128)(2,1)S(1)} %gather_fusion.1) | copy-start | bytes 1572868
  209.2 8.0 copy-start.19
  209.2 6.4 copy-start.13
  211.9 8.6 %copy-start.44 = (f32[512]{0:T(512)}, f32[512]{0:T(512)S(1)}, u32[]{:S(2)}) copy-start(f32[512]{0:T(512)S(1)} %get-tuple-element.160) | copy-start | bytes 6148
  233.1 20.6 %copy-start.45 = (f32[512]{0:T(512)S(1)}, f32[512]{0:T(512)}, u32[]{:S(2)}) copy-start(f32[512]{0:T(512)} %copy-done.44) | copy-start | bytes 6148
  233.1 20.6 %copy-start.51 = (f32[512]{0:T(512)S(1)}, f32[512]{0:T(512)}, u32[]{:S(2)}) copy-start(f32[512]{0:T(512)} %fusion.79) | copy-start | bytes 6148
  257.1 34.7 %copy-start.62 = (f32[128]{0:T(128)}, f32[128]{0:T(128)S(1)}, u32[]{:S(2)}) copy-start(f32[128]{0:T(128)S(1)} %select_select_fusion.1) | copy-start | bytes 1540
  259.1 37.8 %copy-start.63 = (f32[128]{0:T(128)}, f32[128]{0:T(128)S(1)}, u32[]{:S(2)}) copy-start(f32[128]{0:T(128)S(1)} %select_select_fusion) | copy-start | bytes 1540
  260.9 10.2 %copy-start.59 = (pred[128]{0:T(512)(128)(4,1)S(1)}, pred[128]{0:T(512)(128)(4,1)}, u32[]{:S(2)}) copy-start(pred[128]{0:T(512)(128)(4,1)} %copy-done.58) | copy-start | bytes 388
  289.8 534.7 %reduce-scatter.3.cloned.1.call-start = ((), (), s32[]{:S(2)}) async-start(), calls=%async_computation.3 | async-start | bytes 2621440 | tf_op jit(solution)/shard_map/reduce_scatter | solution.py:773
  308.1 6.2 copy-start.26
  311.3 31.1 %copy-start.33 = (f32[2048]{0:T(1024)S(1)}, f32[2048]{0:T(1024)}, u32[]{:S(2)}) copy-start(f32[2048]{0:T(1024)} %param.29) | copy-start | bytes 24580
  311.3 31.1 %copy-start.43 = (f32[512]{0:T(512)S(1)}, f32[512]{0:T(512)}, u32[]{:S(2)}) copy-start(f32[512]{0:T(512)} %copy-done.42) | copy-start | bytes 6148
  316.4 510.4 %reduce-scatter.5.cloned.1.call-start = ((), (), s32[]{:S(2)}) async-start(), calls=%async_computation.6 | async-start | bytes 2621440 | tf_op jit(solution)/shard_map/reduce_scatter | solution.py:899
  318.4 29.5 %copy-start.55 = (f32[512]{0:T(512)S(1)}, f32[512]{0:T(512)}, u32[]{:S(2)}) copy-start(f32[512]{0:T(512)} %get-tuple-element.152) | copy-start | bytes 6148
  342.4 5.6 copy-start.3
  342.4 5.6 copy-start.7
  342.4 5.5 copy-start.12
  368.3 67.5 %copy-start.21 = (f32[512,64]{1,0:T(8,128)S(1)}, f32[512,64]{1,0:T(8,128)}, u32[]{:S(2)}) copy-start(f32[512,64]{1,0:T(8,128)} %copy-done.20) | copy-start | bytes 393220
  438.1 3.0 copy-start.9
  438.1 3.0 copy-start.41
  439.7 5.6 copy-start.35
  439.7 5.6 copy-start.37
  443.8 9.8 %copy-start.47 = (f32[512]{0:T(512)S(1)}, f32[512]{0:T(512)}, u32[]{:S(2)}) copy-start(f32[512]{0:T(512)} %get-tuple-element.148) | copy-start | bytes 6148
  443.8 9.7 %copy-start.48 = (f32[512]{0:T(512)S(1)}, f32[512]{0:T(512)}, u32[]{:S(2)}) copy-start(f32[512]{0:T(512)} %get-tuple-element.169) | copy-start | bytes 6148
  445.3 11.0 %copy-start.4 = (bf16[512,2048]{1,0:T(8,128)(2,1)S(1)}, bf16[512,2048]{1,0:T(8,128)(2,1)}, u32[]{:S(2)}) copy-start(bf16[512,2048]{1,0:T(8,128)(2,1)} %param.20) | copy-start | bytes 6291460
  445.3 11.0 %copy-start.50 = (f32[2048]{0:T(1024)S(1)}, f32[2048]{0:T(1024)}, u32[]{:S(2)}) copy-start(f32[2048]{0:T(1024)} %param.25) | copy-start | bytes 24580
  445.3 11.0 %copy-start.53 = (f32[512]{0:T(512)S(1)}, f32[512]{0:T(512)}, u32[]{:S(2)}) copy-start(f32[512]{0:T(512)} %copy-done.52) | copy-start | bytes 6148
  447.6 8.7 %copy-start.29 = (bf16[512,512]{1,0:T(8,128)(2,1)S(1)}, bf16[512,512]{1,0:T(8,128)(2,1)}, u32[]{:S(2)}) copy-start(bf16[512,512]{1,0:T(8,128)(2,1)} %get-tuple-element.43) | copy-start | bytes 1572868
  456.3 6.8 copy-start.23
  456.3 6.8 copy-start.54
  467.9 3.2 copy-start.14
  467.9 3.2 copy-start.15
  473.5 11.7 %copy-start.28 = (bf16[512,512]{1,0:T(8,128)(2,1)S(1)}, bf16[512,512]{1,0:T(8,128)(2,1)}, u32[]{:S(2)}) copy-start(bf16[512,512]{1,0:T(8,128)(2,1)} %join_heads.1) | copy-start | bytes 1572868
  485.2 5.3 copy-start.25
  808.2 4.3 copy-start.22
  815.0 14.2 %copy-start.1 = (bf16[512,2048]{1,0:T(8,128)(2,1)S(1)}, bf16[512,2048]{1,0:T(8,128)(2,1)}, u32[]{:S(2)}) copy-start(bf16[512,2048]{1,0:T(8,128)(2,1)} %param.28) | copy-start | bytes 6291460
  (11 other events, 22.7 us)
Sparse Core Ops, SparseCore 0:
  137.0 59.1 all-reduce.11
  197.8 22.6 all-gather.1
  289.9 52.4 all-reduce.13
  344.8 31.2 reduce-scatter.2
  465.5 35.3 reduce-scatter.4

commit v3 on v2

--- a/solution.py
+++ b/solution.py
@@ -176,12 +176,16 @@
     return (slice(None), pl.ds(pl.multiple_of(number * HDIM, HDIM), HDIM))
 
 
-def spread_kernel(count, heads, q, k, v, keep, q_all, k_all, v_all, keep_all, *sems):
-    send_one, recv_one, send_two, recv_two, near = sems
+def spread_kernel(
+    count, heads, q, k, v, keep, cot, w_in, q_all, k_all, v_all, keep_all, cot_all, w_split, *sems
+):
+    send_one, recv_one, send_two, recv_two, near, send_cot, recv_cot = sems
+    dp, t = lax.axis_index("dp"), lax.axis_index("tensor")
+    _, _, beside_core, cross, last = tensor_partners()
     z, w, across = line_place(count, heads)
     me = z * across + w
     along, beside = line_devices(count, heads)
-    greet(along + beside)
+    greet(along + beside + [(dp, beside_core), (dp, cross)])
     pairs = ((k, k_all), (v, v_all), (keep, keep_all), (q, q_all))
 
     def piece(item, head):
@@ -207,6 +211,20 @@
             send_sem=send_two.at[item, dz, dw - 1],
             recv_sem=recv_two.at[item, dz, dw - 1],
             device_id=beside[dw - 1],
+            device_id_type=MESH,
+        )
+
+    def columns_of(owner):
+        width = cot.shape[1]
+        return cot_all.at[:, pl.ds(pl.multiple_of(owner * width, width), width)]
+
+    def cot_copy(place, owner):
+        return pltpu.make_async_remote_copy(
+            src_ref=columns_of(owner) if place == 2 else cot,
+            dst_ref=columns_of(owner),
+            send_sem=send_cot.at[place],
+            recv_sem=recv_cot.at[place],
+            device_id=(dp, cross if place == 1 else beside_core),
             device_id_type=MESH,
         )
 
@@ -223,6 +241,22 @@
         copy = pltpu.make_async_copy(piece(item, z), own, near.at[item])
         copy.start()
         local.append(copy)
+    cot_copy(0, t).start()
+    cot_copy(1, t).start()
+    copy = pltpu.make_async_copy(cot, columns_of(t), near.at[4])
+    copy.start()
+    local.append(copy)
+
+    @pl.loop(0, w_in.shape[0])
+    def _(e):
+        @pl.loop(0, w_in.shape[1] // 128)
+        def _(turn):
+            here = pl.ds(pl.multiple_of(turn * 128, 128), 128)
+            w_split[e, 0, here, :] = w_in[e, here, 0, :]
+            w_split[e, 1, here, :] = w_in[e, here, 1, :]
+
+    cot_copy(1, cross).wait_recv()
+    cot_copy(2, cross).start()
     for item, dz in first:
         first_copy(item, dz).wait_recv()
         if item < 3:
@@ -234,30 +268,48 @@
         first_copy(item, dz).wait_send()
     for dz, item, dw in second:
         second_copy(item, dz, dw).wait_send()
+    cot_copy(0, beside_core).wait_recv()
+    cot_copy(2, last).wait_recv()
+    for place in range(3):
+        cot_copy(place, cross if place == 2 else t).wait_send()
     for copy in local:
         copy.wait()
 
 
-def spread_heads(q, k, v, keep, count, heads, number):
+def spread_heads(q, k, v, keep, cot, w_in, count, heads, number):
     rows = q.shape[0]
     across = count // heads
     sem = pltpu.SemaphoreType.DMA
-    shapes = [(heads, rows, HDIM), (count, rows, HDIM), (count, rows, HDIM), (count, *keep.shape)]
+    window, deep, _, units = w_in.shape
+    shapes = [
+        (heads, rows, HDIM),
+        (count, rows, HDIM),
+        (count, rows, HDIM),
+        (count, *keep.shape),
+        (rows, 4 * cot.shape[1]),
+        (window, 2, deep, units),
+    ]
     return pl.pallas_call(
         functools.partial(spread_kernel, count, heads),
         out_shape=[jax.ShapeDtypeStruct(shape, jnp.bfloat16) for shape in shapes],
-        in_specs=[pl.BlockSpec(memory_space=pl.ANY)] * 4,
-        out_specs=[pl.BlockSpec(memory_space=pl.ANY)] * 4,
+        in_specs=[pl.BlockSpec(memory_space=pl.ANY)] * 5
+        + [pl.BlockSpec(memory_space=pltpu.VMEM)],
+        out_specs=[pl.BlockSpec(memory_space=pl.ANY)] * 5
+        + [pl.BlockSpec(memory_space=pltpu.VMEM)],
         scratch_shapes=[
             sem((4, heads - 1)),
             sem((4, heads - 1)),
             sem((3, heads, across - 1)),
             sem((3, heads, across - 1)),
-            sem((4,)),
+            sem((5,)),
+            sem((3,)),
+            sem((3,)),
         ],
-        compiler_params=pltpu.CompilerParams(collective_id=number, has_side_effects=True),
+        compiler_params=pltpu.CompilerParams(
+            collective_id=number, has_side_effects=True, vmem_limit_bytes=40 << 20
+        ),
         name="spread_heads",
-    )(q, k, v, keep)
+    )(q, k, v, keep, cot, w_in)
 
 
 def swap_kernel(count, heads, join, source, result, send_sem, recv_sem, near):
@@ -610,6 +662,329 @@
     w = lax.rem(lax.axis_index("dp"), count // heads)
     mine = lax.dynamic_slice_in_dim(table, w, 1, 2).reshape(3, heads * per)
     return inverse, mine[0], mine[1], mine[2]
+
+
+def tensor_partners():
+    t = lax.axis_index("tensor")
+    pair, side = t // 2, lax.rem(t, 2)
+    near = t + 1 - 2 * side
+    cross = t + 2 - 4 * pair
+    return pair, side, near, cross, 3 - t
+
+
+def tensor_sum_kernel(chunks, source, extra, result, extra_all, came, half_sum, crossed, *sems):
+    send_sem, recv_sem, extra_send, extra_recv = sems
+    dp, t = lax.axis_index("dp"), lax.axis_index("tensor")
+    _, side, near, cross, last = tensor_partners()
+    greet([(dp, near), (dp, cross), (dp, last)])
+    half = source.shape[0] // 2
+    piece = half // chunks
+
+    def lines(which, j):
+        return pl.ds(pl.multiple_of(which * half + j * piece, piece), piece)
+
+    def copy(stage, j, source_ref, target_ref, device):
+        return pltpu.make_async_remote_copy(
+            src_ref=source_ref,
+            dst_ref=target_ref,
+            send_sem=send_sem.at[stage, j],
+            recv_sem=recv_sem.at[stage, j],
+            device_id=(dp, device),
+            device_id_type=MESH,
+        )
+
+    def near_copy(j):
+        return copy(0, j, source.at[lines(1 - side, j)], came.at[j], near)
+
+    def cross_copy(j):
+        return copy(1, j, half_sum.at[j], crossed.at[j], cross)
+
+    def last_copy(j, which):
+        return copy(2, j, result.at[lines(which, j)], result.at[lines(which, j)], near)
+
+    def extra_copy(place, device):
+        return pltpu.make_async_remote_copy(
+            src_ref=extra,
+            dst_ref=extra_all.at[t],
+            send_sem=extra_send.at[place],
+            recv_sem=extra_recv.at[place],
+            device_id=(dp, device),
+            device_id_type=MESH,
+        )
+
+    for j in range(chunks):
+        near_copy(j).start()
+    for place, device in enumerate((near, cross, last)):
+        extra_copy(place, device).start()
+    extra_all[t] = extra[...]
+    add = lambda a, b: (a[...].astype(jnp.float32) + b[...].astype(jnp.float32)).astype(
+        jnp.bfloat16
+    )
+    for j in range(chunks):
+        near_copy(j).wait_recv()
+        half_sum[j] = add(source.at[lines(side, j)], came.at[j])
+        cross_copy(j).start()
+    for j in range(chunks):
+        cross_copy(j).wait_recv()
+        result[lines(side, j), :] = add(half_sum.at[j], crossed.at[j])
+        last_copy(j, side).start()
+    for j in range(chunks):
+        last_copy(j, 1 - side).wait_recv()
+    for place, device in enumerate((near, cross, last)):
+        extra_copy(place, device).wait()
+    for j in range(chunks):
+        near_copy(j).wait_send()
+        cross_copy(j).wait_send()
+        last_copy(j, side).wait_send()
+
+
+def tensor_sum(source, extra, number, chunks):
+    rows, columns = source.shape
+    block = pltpu.VMEM((chunks, rows // 2 // chunks, columns), jnp.bfloat16)
+    vmem = pl.BlockSpec(memory_space=pltpu.VMEM)
+    sem = pltpu.SemaphoreType.DMA
+    return pl.pallas_call(
+        functools.partial(tensor_sum_kernel, chunks),
+        out_shape=[
+            jax.ShapeDtypeStruct(source.shape, jnp.bfloat16),
+            jax.ShapeDtypeStruct((4, *extra.shape), jnp.float32),
+        ],
+        in_specs=[vmem] * 2,
+        out_specs=[vmem] * 2,
+        scratch_shapes=[
+            block,
+            block,
+            block,
+            sem((3, chunks)),
+            sem((3, chunks)),
+            sem((3,)),
+            sem((3,)),
+        ],
+        compiler_params=pltpu.CompilerParams(
+            collective_id=number, has_side_effects=True, vmem_limit_bytes=60 << 20
+        ),
+        name="tensor_sum",
+    )(source, extra)
+
+
+def tensor_share_kernel(chunks, source, result, came, pair_sum, crossed, *sems):
+    send_sem, recv_sem = sems
+    dp = lax.axis_index("dp")
+    pair, side, near, cross, last = tensor_partners()
+    greet([(dp, near), (dp, cross)])
+    rows, width = result.shape
+    piece = rows // chunks
+
+    def part(j, owner):
+        return (
+            pl.ds(j * piece, piece),
+            pl.ds(pl.multiple_of(owner * width, width), width),
+        )
+
+    def copy(stage, j, source_ref, target_ref, device):
+        return pltpu.make_async_remote_copy(
+            src_ref=source_ref,
+            dst_ref=target_ref,
+            send_sem=send_sem.at[stage, j],
+            recv_sem=recv_sem.at[stage, j],
+            device_id=(dp, device),
+            device_id_type=MESH,
+        )
+
+    def near_copy(j, where):
+        owner = near if where else last
+        return copy(where, j, source.at[part(j, owner)], came.at[where, j], near)
+
+    def cross_copy(j):
+        return copy(2, j, pair_sum.at[j], crossed.at[j], cross)
+
+    for j in range(chunks):
+        for where in (0, 1):
+            near_copy(j, where).start()
+    f32 = jnp.float32
+    for j in range(chunks):
+        near_copy(j, 0).wait_recv()
+        pair_sum[j] = (source[part(j, cross)].astype(f32) + came[0, j].astype(f32)).astype(
+            jnp.bfloat16
+        )
+        cross_copy(j).start()
+    t = lax.axis_index("tensor")
+    for j in range(chunks):
+        near_copy(j, 1).wait_recv()
+        cross_copy(j).wait_recv()
+        total = source[part(j, t)].astype(f32) + came[1, j].astype(f32)
+        result[pl.ds(j * piece, piece), :] = (total + crossed[j].astype(f32)).astype(jnp.bfloat16)
+    for j in range(chunks):
+        near_copy(j, 0).wait_send()
+        near_copy(j, 1).wait_send()
+        cross_copy(j).wait_send()
+
+
+def tensor_share(source, number, chunks):
+    rows, columns = source.shape
+    width = columns // 4
+    piece = rows // chunks
+    vmem = pl.BlockSpec(memory_space=pltpu.VMEM)
+    sem = pltpu.SemaphoreType.DMA
+    return pl.pallas_call(
+        functools.partial(tensor_share_kernel, chunks),
+        out_shape=jax.ShapeDtypeStruct((rows, width), jnp.bfloat16),
+        in_specs=[vmem],
+        out_specs=vmem,
+        scratch_shapes=[
+            pltpu.VMEM((2, chunks, piece, width), jnp.bfloat16),
+            pltpu.VMEM((chunks, piece, width), jnp.bfloat16),
+            pltpu.VMEM((chunks, piece, width), jnp.bfloat16),
+            sem((3, chunks)),
+            sem((3, chunks)),
+        ],
+        compiler_params=pltpu.CompilerParams(
+            collective_id=number, has_side_effects=True, vmem_limit_bytes=60 << 20
+        ),
+        name="tensor_share",
+    )(source)
+
+
+def experts_kernel(
+    x,
+    branch,
+    gain,
+    router,
+    ids,
+    cot,
+    w_in,
+    w_out,
+    slots,
+    row_grad,
+    mixed,
+    dots,
+    grad_in,
+    grad_out,
+    normed,
+    rows,
+    cot_rows,
+    part_grad,
+):
+    tokens, width = x.shape
+    hidden_units = w_out.shape[1]
+    f32, low = jnp.float32, jnp.bfloat16
+    tile = 512
+
+    @pl.loop(0, tokens // 64)
+    def _(turn):
+        here = pl.ds(pl.multiple_of(turn * 64, 64), 64)
+        hidden = x[here, :].astype(f32) + branch[here, :].astype(f32)
+        scale = lax.rsqrt(jnp.mean(hidden * hidden, axis=-1, keepdims=True) + EPSILON)
+        normed[here, :] = (hidden * scale * gain[...]).astype(low)
+
+    before = (
+        lax.broadcasted_iota(jnp.int32, (tokens, tokens), 0)
+        <= lax.broadcasted_iota(jnp.int32, (tokens, tokens), 1)
+    ).astype(low)
+
+    @pl.loop(0, w_in.shape[0])
+    def _(e):
+        chosen = jnp.max((ids[...] == e).astype(f32), axis=0, keepdims=True)
+        rank = jnp.dot(
+            jnp.broadcast_to(chosen, (8, tokens)).astype(low), before, preferred_element_type=f32
+        )[0:1]
+        slot = lax.broadcasted_iota(jnp.int32, (CAP, tokens), 0).astype(f32) + 1.0
+        picked = jnp.where((rank == slot) & (chosen > 0.0), 1.0, 0.0)
+        live = jnp.sum(picked, axis=1, keepdims=True)
+        picked = picked.astype(low)
+        slots[e] = picked
+
+        @pl.loop(0, width // tile)
+        def _(j):
+            here = pl.ds(pl.multiple_of(j * tile, tile), tile)
+            rows[:, here] = jnp.dot(picked, normed[:, here], preferred_element_type=f32).astype(low)
+            cot_rows[:, here] = jnp.dot(picked, cot[:, here], preferred_element_type=f32).astype(
+                low
+            )
+
+        logits = across_rows(rows[...], router[...])
+        shifted = jnp.exp(logits - jnp.max(logits, axis=-1, keepdims=True))
+        expert = lax.broadcasted_iota(jnp.int32, logits.shape, 1)
+        gate = (
+            jnp.sum(jnp.where(expert == e, shifted, 0.0), axis=-1, keepdims=True)
+            / jnp.sum(shifted, axis=-1, keepdims=True)
+            * live
+        )
+        into = jnp.dot(rows[...], w_in[e, 0], preferred_element_type=f32)
+        up = jnp.dot(rows[...], w_in[e, 1], preferred_element_type=f32)
+        sig = 1.0 / (1.0 + jnp.exp(-into))
+        silu = into * sig
+        active = (silu * up).astype(low)
+
+        def forward(j, state):
+            dot_sum, act_grad = state
+            here = pl.ds(pl.multiple_of(j * tile, tile), tile)
+            out = jnp.dot(active, w_out[e, :, here], preferred_element_type=f32)
+            mixed[e, :, here] = (gate * out).astype(low)
+            wide = cot_rows[:, here].astype(f32)
+            grad = (gate * wide).astype(low)
+            part_grad[:, here] = grad
+            return (
+                dot_sum + jnp.sum(wide * out, axis=-1, keepdims=True),
+                act_grad + across_rows(grad, w_out[e, :, here]),
+            )
+
+        dot_sum, act_grad = lax.fori_loop(
+            0,
+            width // tile,
+            forward,
+            (jnp.zeros((CAP, 1), f32), jnp.zeros((CAP, hidden_units), f32)),
+        )
+        dots[e] = jnp.broadcast_to(dot_sum * live, (CAP, 128)).T[0:8]
+        into_grad = (act_grad * up * (sig * (1.0 + into * (1.0 - sig)))).astype(low)
+        up_grad = (act_grad * silu).astype(low)
+        active_turned = active.astype(f32).T.astype(low)
+
+        @pl.loop(0, width // tile)
+        def _(j):
+            here = pl.ds(pl.multiple_of(j * tile, tile), tile)
+            row_grad[e, :, here] = (
+                across_rows(into_grad, w_in[e, 0, here, :])
+                + across_rows(up_grad, w_in[e, 1, here, :])
+            ).astype(low)
+            grad_out[e, :, here] = jnp.dot(
+                active_turned, part_grad[:, here], preferred_element_type=f32
+            ).astype(low)
+            turned = rows[:, here].astype(f32).T.astype(low)
+            grad_in[e, here, 0:hidden_units] = jnp.dot(
+                turned, into_grad, preferred_element_type=f32
+            ).astype(low)
+            grad_in[e, here, hidden_units:] = jnp.dot(
+                turned, up_grad, preferred_element_type=f32
+            ).astype(low)
+
+
+def experts_call(x, branch, gain, router, ids, cot, w_in, w_out):
+    tokens, width = x.shape
+    window, hidden_units = w_out.shape[:2]
+    shape, low = jax.ShapeDtypeStruct, jnp.bfloat16
+    vmem = pl.BlockSpec(memory_space=pltpu.VMEM)
+    return pl.pallas_call(
+        experts_kernel,
+        out_shape=[
+            shape((window, CAP, tokens), low),
+            shape((window, CAP, width), low),
+            shape((window, CAP, width), low),
+            shape((window, 8, CAP), jnp.float32),
+            shape((window, width, 2 * hidden_units), low),
+            shape((window, hidden_units, width), low),
+        ],
+        in_specs=[vmem] * 8,
+        out_specs=[vmem] * 6,
+        scratch_shapes=[
+            pltpu.VMEM((tokens, width), low),
+            pltpu.VMEM((CAP, width), low),
+            pltpu.VMEM((CAP, width), low),
+            pltpu.VMEM((CAP, width), low),
+        ],
+        compiler_params=pltpu.CompilerParams(vmem_limit_bytes=60 << 20),
+        name="experts",
+    )(x, branch, gain, router, ids, cot, w_in, w_out)
 
 
 def row_scale(values):
@@ -712,11 +1087,13 @@
     v_low = values_here.astype(jnp.bfloat16)
     keep_here = pad_mask.astype(jnp.bfloat16)
     dp_count = lax.axis_size("dp")
-    q_line, k_all, v_all, keep_all = spread_heads(
+    q_line, k_all, v_all, keep_all, cot_low, w_split = spread_heads(
         q_rot.reshape(rows_here, local_width),
         k_rot.reshape(rows_here, local_width),
         v_low,
         jnp.broadcast_to(keep_here[None], (8, rows_here)),
+        cotangent,
+        expert_in,
         dp_count,
         heads_here,
         1,
@@ -734,94 +1111,40 @@
     attended_low = swap_line(
         line_out.reshape(heads_here, rows_here, HDIM), dp_count, heads_here, True, 2
     )
-    branch = lax.psum(
+    branch_low, _ = tensor_sum(
         jnp.dot(attended_low, w_out, preferred_element_type=jnp.float32).astype(jnp.bfloat16),
-        "tensor",
-    ).astype(jnp.float32)
-    hidden = inputs + branch
+        jnp.zeros((8, 128), jnp.float32),
+        5,
+        4,
+    )
+    slots, slot_grad, slot_mixed, slot_dots, expert_in_grad, expert_out_grad = experts_call(
+        tokens,
+        branch_low,
+        ffn_gain[None],
+        jnp.transpose(router),
+        jnp.transpose(expert_ids),
+        cot_low,
+        w_split,
+        expert_out,
+    )
+    slot_grad, dots_all = tensor_sum(
+        slot_grad.reshape(WIN * CAP, model_width), slot_dots.reshape(WIN * 8, CAP), 6, 2
+    )
+    flat_slots = slots.reshape(WIN * CAP, rows_here)
+    mixture_grad = jnp.einsum("ct,cd->td", flat_slots, slot_grad, preferred_element_type=jnp.float32)
+    slot_dots = jnp.sum(dots_all, axis=0).reshape(WIN, 8, CAP)[:, 0]
+    gate_grad = jnp.transpose(
+        jnp.sum(jnp.where(slots > 0, slot_dots[:, :, None], 0.0), axis=1)
+    )
+    hidden = inputs + branch_low.astype(jnp.float32)
     h_scale = row_scale(hidden)
     normed = (hidden * h_scale * ffn_gain).astype(jnp.bfloat16)
     logits = jnp.dot(normed, router, preferred_element_type=jnp.float32)
     router_probs = jax.nn.softmax(logits, axis=-1)
-    window_ids = jnp.arange(WIN, dtype=jnp.int32)
-    chosen = jnp.any(expert_ids[:, :, None] == window_ids[None, None, :], axis=1)
-    chosen_float = chosen.astype(jnp.float32)
-    gate_values = router_probs[:, :WIN] * chosen_float
-    slot_ids = jnp.arange(CAP, dtype=jnp.int32)
-    token_ids = jnp.arange(rows_here, dtype=jnp.int32)
-    mixture = jnp.zeros((rows_here, model_width), jnp.float32)
-    saved_slots = []
-    for expert in range(WIN):
-        picked = chosen[:, expert]
-        slot_rank = jnp.cumsum(picked.astype(jnp.int32)) - 1
-        slot_table = (slot_rank[None, :] == slot_ids[:, None]) & picked[None, :]
-        slot_token = jnp.sum(jnp.where(slot_table, token_ids[None, :], 0), axis=1)
-        slot_live = jnp.any(slot_table, axis=1).astype(jnp.float32)
-        gathered_rows = jnp.take(normed, slot_token, axis=0)
-        gate_up = jnp.dot(
-            gathered_rows,
-            expert_in[expert].reshape(model_width, 2 * local_ff),
-            preferred_element_type=jnp.float32,
-        ).reshape(CAP, 2, local_ff)
-        active = (jax.nn.silu(gate_up[:, 0]) * gate_up[:, 1]).astype(jnp.bfloat16)
-        expert_part = jnp.dot(active, expert_out[expert], preferred_element_type=jnp.float32)
-        slot_gate = jnp.take(gate_values[:, expert], slot_token) * slot_live
-        mixture = mixture.at[slot_token].add(slot_gate[:, None] * expert_part)
-        saved_slots.append(
-            (slot_token, slot_live, gathered_rows, gate_up, active, expert_part, slot_gate)
-        )
-    mixture_share = lax.psum_scatter(
-        mixture.astype(jnp.bfloat16), "tensor", scatter_dimension=1, tiled=True
-    ).astype(jnp.float32)
     hidden_share = lax.dynamic_slice_in_dim(hidden, feature_start, local_width, 1)
-    output = (hidden_share + mixture_share).astype(jnp.bfloat16)
-    cot_full = lax.all_gather(cotangent, "tensor", axis=1, tiled=True).astype(jnp.float32)
-    mixture_grad = jnp.zeros((rows_here, model_width), jnp.float32)
-    gate_columns = []
-    expert_in_list = []
-    expert_out_list = []
-    for expert in range(WIN):
-        slot_token, slot_live, gathered_rows, gate_up, active, expert_part, slot_gate = saved_slots[
-            expert
-        ]
-        cot_rows = jnp.take(cot_full, slot_token, axis=0)
-        part_grad = (slot_gate[:, None] * cot_rows).astype(jnp.bfloat16)
-        slot_dots = jnp.sum(cot_rows * expert_part, axis=-1) * slot_live
-        gate_columns.append(jnp.zeros((rows_here,), jnp.float32).at[slot_token].add(slot_dots))
-        expert_out_list.append(
-            jnp.einsum("cf,cd->fd", active, part_grad, preferred_element_type=jnp.float32)
-        )
-        active_grad = jnp.einsum(
-            "cd,fd->cf", part_grad, expert_out[expert], preferred_element_type=jnp.float32
-        )
-        _, silu_pull = jax.vjp(
-            lambda gate_in, up_in: jax.nn.silu(gate_in) * up_in, gate_up[:, 0], gate_up[:, 1]
-        )
-        gate_in_grad, up_in_grad = silu_pull(active_grad)
-        pair_grad = (
-            jnp.stack([gate_in_grad, up_in_grad], axis=1)
-            .astype(jnp.bfloat16)
-            .reshape(CAP, 2 * local_ff)
-        )
-        expert_in_list.append(
-            jnp.einsum(
-                "cd,cf->df", gathered_rows, pair_grad, preferred_element_type=jnp.float32
-            ).reshape(model_width, 2, local_ff)
-        )
-        row_grad = jnp.einsum(
-            "cf,df->cd",
-            pair_grad,
-            expert_in[expert].reshape(model_width, 2 * local_ff),
-            preferred_element_type=jnp.float32,
-        )
-        mixture_grad = mixture_grad.at[slot_token].add(row_grad)
-    gate_grad = jnp.stack(gate_columns, axis=1)
-    mixture_grad, gate_grad = (
-        lax.psum(mixture_grad.astype(jnp.bfloat16), "tensor").astype(jnp.float32),
-        lax.psum(gate_grad.astype(jnp.bfloat16), "tensor").astype(jnp.float32),
-    )
+    cot_full = cot_low.astype(jnp.float32)
     probs_grad = jnp.concatenate(
-        [gate_grad * chosen_float, jnp.zeros((rows_here, router.shape[1] - WIN), jnp.float32)],
+        [gate_grad, jnp.zeros((rows_here, router.shape[1] - WIN), jnp.float32)],
         axis=1,
     )
     logit_grad = (
@@ -838,8 +1161,6 @@
         jnp.sum(normed_grad * hidden * h_scale, axis=0), feature_start, local_width, 0
     )
     hidden_grad = cot_full + norm_back(hidden, h_scale, ffn_gain, normed_grad, model_width)
-    expert_in_grad = jnp.stack(expert_in_list)
-    expert_out_grad = jnp.stack(expert_out_list)
     branch_grad = hidden_grad.astype(jnp.bfloat16)
     out_grad = jnp.einsum(
         "tc,td->cd", attended_low, branch_grad, preferred_element_type=jnp.float32
@@ -895,14 +1216,26 @@
     )
     input_part = norm_back(inputs, x_scale, attn_gain, normed_in_grad, model_width)
     gain_part = jnp.sum(normed_in_grad * inputs * x_scale, axis=0)
-    input_sum, attn_gain_grad = (
-        lax.psum_scatter(
-            input_part.astype(jnp.bfloat16), "tensor", scatter_dimension=1, tiled=True
-        ).astype(jnp.float32),
-        lax.psum_scatter(
-            gain_part.astype(jnp.bfloat16), "tensor", scatter_dimension=0, tiled=True
-        ).astype(jnp.float32),
-    )
+    shares = tensor_share(
+        jnp.concatenate(
+            [
+                input_part.astype(jnp.bfloat16),
+                slot_mixed.reshape(WIN * CAP, model_width),
+                jnp.broadcast_to(gain_part.astype(jnp.bfloat16)[None], (32, model_width)),
+            ]
+        ),
+        7,
+        2,
+    )
+    input_sum = shares[:rows_here].astype(jnp.float32)
+    mixture_share = jnp.einsum(
+        "ct,cd->td",
+        flat_slots,
+        shares[rows_here : rows_here + WIN * CAP],
+        preferred_element_type=jnp.float32,
+    )
+    output = (hidden_share + mixture_share).astype(jnp.bfloat16)
+    attn_gain_grad = shares[rows_here + WIN * CAP].astype(jnp.float32)
     input_grad = (
         lax.dynamic_slice_in_dim(hidden_grad, feature_start, local_width, 1) + input_sum
     ).astype(jnp.bfloat16)
@@ -921,8 +1254,8 @@
         [
             jnp.transpose(qkv_grad, (1, 0, 2)).astype(low),
             out_grad.astype(low)[None],
-            expert_in_grad.reshape(WIN, model_width, 2 * local_ff).astype(low),
-            expert_out_grad.astype(low),
+            expert_in_grad,
+            expert_out_grad,
             small[None],
         ],
         dp_count,
@@ -930,7 +1263,7 @@
     )
     qkv_grad = jnp.transpose(qkv_sum.astype(jnp.float32), (1, 0, 2))
     out_grad = out_sum[0].astype(jnp.float32)
-    expert_in_grad = in_sum.astype(jnp.float32).reshape(expert_in_grad.shape)
+    expert_in_grad = in_sum.astype(jnp.float32).reshape(expert_in.shape)
     expert_out_grad = exp_sum.astype(jnp.float32)
     router_rows = router_grad.size // 256
     small_sum = small_sum[0].astype(jnp.float32)

time: 845 us -> 731 us (0.87)
  Pallas kernels: 451 us -> 556 us
  waiting for transfers between devices: 64.2 us -> 0 us
  other arithmetic: 118 us -> 57.7 us
  matrix products: 71.8 us -> 39.7 us
  local copies, waits for them, and re-layouts: 88 us -> 56.9 us
  between operations: 15.8 us -> 1.8 us
  blocking collectives: 27.1 us -> 14.2 us
    pallas_call x0 -> x4, Pallas kernels: none -> 97.7 us  [the longest x2 51.1 us: tensor_sum(): pl.pallas_call(functools.partial(tensor_sum_kernel, chunks), out_shape=[j...]
    psum x2 -> x0, waiting for transfers between devices: 60.2 us -> none  [the longest x1 36.2 us: body(): lax.psum(jnp.dot(attended_low, w_out, preferred_element_type=jnp.float32)...]
    scatter-add x6 -> x0, other arithmetic: 28.6 us -> none  [the longest x2 12.5 us: body(): mixture = mixture.at[slot_token].add(slot_gate[:, None] * expert_part)]
    dot_general x12 -> x2, matrix products: 31.5 us -> 4.62 us  [the longest x1 2.44 us: body(): jnp.einsum('ct,cd->td', flat_slots, shares[rows_here:rows_here + WIN * CA...]
    gather x6 -> x0, local copies, waits for them, and re-layouts: 18.1 us -> none  [the longest x2 8.49 us: body(): cot_rows = jnp.take(cot_full, slot_token, axis=0)]
    convert_element_type x6 -> x0, other arithmetic: 15.5 us -> none  [the longest x1 4.13 us: body(): lax.all_gather(cotangent, 'tensor', axis=1, tiled=True).astype(jnp.float32)]
    unnamed x154 -> x76, local copies, waits for them, and re-layouts: 22.5 us -> 24 us
  transfers between devices with their start and end apart: 5 -> 0, of which waited for: 3 -> 0; matrix products, arithmetic and copies ran while one was open for 20% -> 0% of each run, Pallas kernels for 45% -> 0%
where the time goes in v3:
time: 731 us; the launch traced here: 727 us
  Pallas kernels  556 us (76%)
  other arithmetic  57.7 us (8%)
  local copies, waits for them, and re-layouts  56.9 us (8%)
  matrix products  39.7 us (5%)
  blocking collectives  14.2 us (2%)
    pallas_call x1, Pallas kernels, ring_sum(): pl.pallas_call(functools.partial(ring_kernel, count, parts), out_shape=[j...  299 us
    pallas_call x2, Pallas kernels, tensor_sum(): pl.pallas_call(functools.partial(tensor_sum_kernel, chunks), out_shape=[j...  51.1 us
    pallas_call x1, Pallas kernels, spread_heads(): pl.pallas_call(functools.partial(spread_kernel, count, heads), out_shape=...  41.1 us
    pallas_call x1, Pallas kernels, return_heads(): pl.pallas_call(functools.partial(return_kernel, count, heads), out_shape=...  40.9 us
    pallas_call x2, Pallas kernels, swap_line(): pl.pallas_call(functools.partial(swap_kernel, count, heads, join), out_sh...  33.5 us
    pallas_call x1, Pallas kernels, tensor_share(): pl.pallas_call(functools.partial(tensor_share_kernel, chunks), out_shape=...  25.4 us
    unnamed x76, local copies, waits for them, and re-layouts  24 us
    pallas_call x1, Pallas kernels, back(): pl.pallas_call(attend_back_kernel, out_shape=[shape((rows, HDIM), low), s...  23.9 us

profile of v3, /device:TPU:0, one launch (start us, length us, event | category | flops | bytes accessed | tf_op | source)
XLA Modules:
  0.0 726.7 jit_solution(17096919846062302660)
XLA Ops:
  0.7 1.0 reduce-window.8
  3.0 1.3 select_reduce_fusion.2.inverse
  5.0 2.1 fusion.2
  9.6 1.0 multiply_cosine_fusion
  10.6 8.8 %copy.38 = bf16[2048,3,512]{0,2,1:T(8,128)(2,1)} copy(bf16[2048,3,512]{2,0,1:T(8,128)(2,1)} %param.20) | data formatting | bytes 12582912 | tf_op args[6]
  19.3 6.5 fusion
  25.9 1.7 copy-done.14
  27.8 8.5 %all-reduce.7 = (f32[512]{0:T(512)S(1)}, f32[512]{0:T(512)S(1)}) all-reduce(f32[512]{0:T(512)S(1)} %get-tuple-element.105, f32[512]{0:T(512)S(1)} %get-tuple-element.104), channel_id=1, replica_groups=mesh['dp'=8,'tensor'=4] {'tensor'}, use_global_device_ids=true, to_apply=%region_6.7 | all-reduce | flops 1024 | bytes 8192 | tf_op jit(solution)/shard_map/psum | solution.py:1078
  36.4 1.3 fusion.25.v
  37.7 3.0 fusion.52
  40.7 2.5 squeeze.25
  43.2 2.6 squeeze.23
  45.8 2.5 multiply_multiply_fusion.1
  48.3 2.5 multiply_multiply_fusion
  50.9 1.6 subtract_convert_fusion.2
  54.2 41.1 %spread_heads.1 = (bf16[4,512,128]{2,1,0:T(8,128)(2,1)S(1)}, bf16[8,512,128]{2,1,0:T(8,128)(2,1)S(1)}, bf16[8,512,128]{2,1,0:T(8,128)(2,1)S(1)}, bf16[8,8,512]{2...) custom-call(bf16[512,512]{1,0:T(8,128)(2,1)S(1)} %bitcast.141, ...), custom_call_target="tpu_custom_call" | custom-call | tf_op jit(solution)/shard_map/spread_heads/pallas_call | solution.py:292
  95.3 1.3 copy-done.2
  96.6 2.0 copy-done.4
  98.6 1.0 copy-done.5
  99.6 1.1 copy-done.6
  103.9 20.0 %attend.1 = (f32[2048,128]{1,0:T(8,128)}, bf16[2048,128]{1,0:T(8,128)(2,1)}, f32[16,8,128]{2,1,0:T(8,128)}) custom-call(s32[32]{0:T(128)} %select_reduce_fusion.2.inverse, s32[16]{0:T(128)} %squeeze.27.first, s32[16]{0:T(128)} %squeeze.28.own, s32[16]{0:T(128)} %squeeze.29.stop, bf16[2048,128]{1,0:T(8,128)(2,1)} %bitcast.142, bf16[4096,128]{1,0:T(8,128)(2,1)} %bitcast.136, ...), custom_call_target="tpu_custom_call" | custom-call | tf_op jit(solution)/shard_map/attend/pallas_call | solution.py:613
  124.0 18.0 %join_heads.1 = bf16[512,512]{1,0:T(8,128)(2,1)} custom-call(bf16[4,512,128]{2,1,0:T(8,128)(2,1)} %bitcast.157), custom_call_target="tpu_custom_call" | custom-call | tf_op jit(solution)/shard_map/join_heads/pallas_call | solution.py:348
  141.9 3.6 convolution_convert_fusion.1.source
  146.2 31.4 %tensor_sum.2 = (bf16[512,2048]{1,0:T(8,128)(2,1)}, f32[4,8,128]{2,1,0:T(8,128)}) custom-call(bf16[512,2048]{1,0:T(8,128)(2,1)} %convolution_convert_fusion.1.source, f32[8,128]{1,0:T(8,128)} %broadcast_in_dim.101.extra), custom_call_target="tpu_custom_call" | custom-call | tf_op jit(solution)/shard_map/tensor_sum/pallas_call | solution.py:746
  177.6 3.1 multiply_reduce_fusion.2
  181.1 1.1 multiply_convert_fusion
  182.2 1.3 copy-done.18
  184.4 21.2 %experts.1 = (bf16[2,128,512]{2,1,0:T(8,128)(2,1)}, bf16[2,128,2048]{2,1,0:T(8,128)(2,1)}, bf16[2,128,2048]{2,1,0:T(8,128)(2,1)}, f32[2,8,128]{2,1,0:T(8,128)}, ...) custom-call(bf16[512,2048]{1,0:T(8,128)(2,1)} %x.13, bf16[512,2048]{1,0:T(8,128)(2,1)} %get-tuple-element.44.branch, ...), custom_call_target="tpu_custom_call" | custom-call | tf_op jit(solution)/shard_map/experts/pallas_call | solution.py:967
  205.5 19.7 %tensor_sum.3 = (bf16[256,2048]{1,0:T(8,128)(2,1)}, f32[4,16,128]{2,1,0:T(8,128)}) custom-call(bf16[256,2048]{1,0:T(8,128)(2,1)} %bitcast.155, f32[16,128]{1,0:T(8,128)} %bitcast.173), custom_call_target="tpu_custom_call" | custom-call | tf_op jit(solution)/shard_map/tensor_sum/pallas_call | solution.py:746
  226.0 1.1 select_reduce_fusion
  227.2 1.2 convolution_convert_fusion.3
  228.7 2.2 fusion.55
  231.4 1.8 multiply_reduce_fusion
  233.3 3.1 subtract_add_fusion
  236.4 2.0 copy-done.19
  238.4 2.1 convolution_convert_fusion.2.source
  240.6 15.5 %part_heads.1 = bf16[4,512,128]{2,1,0:T(8,128)(2,1)} custom-call(bf16[512,512]{1,0:T(8,128)(2,1)} %convolution_convert_fusion.2.source), custom_call_target="tpu_custom_call" | custom-call | tf_op jit(solution)/shard_map/part_heads/pallas_call | solution.py:348
  256.1 23.9 %attend_back.1 = (bf16[2048,128]{1,0:T(8,128)(2,1)}, bf16[4096,128]{1,0:T(8,128)(2,1)}, bf16[4096,128]{1,0:T(8,128)(2,1)}) custom-call(s32[32]{0:T(128)} %select_reduce_fusion.2.inverse, s32[16]{0:T(128)} %squeeze.27.first, s32[16]{0:T(128)} %squeeze.28.own, s32[16]{0:T(128)} %squeeze.29.stop, bf16[2048,128]{1,0:T(8,128)(2,1)} %bitcast.143, ...), custom_call_target="tpu_custom_call" | custom-call | tf_op jit(solution)/shard_map/attend_back/pallas_call | solution.py:628
  279.9 40.9 %return_heads.1 = (bf16[512,512]{1,0:T(8,128)(2,1)}, bf16[512,512]{1,0:T(8,128)(2,1)}, bf16[512,512]{1,0:T(8,128)(2,1)}) custom-call(bf16[4,512,128]{2,1,0:T(8,128)(2,1)} %bitcast.156, bf16[8,512,128]{2,1,0:T(8,128)(2,1)} %bitcast.153, bf16[8,512,128]{2,1,0:T(8,128)(2,1)} %bitcast.154), custom_call_target="tpu_custom_call" | custom-call | tf_op jit(solution)/shard_map/return_heads/pallas_call | solution.py:449
  320.8 1.4 reshape.536
  322.2 1.4 reshape.538
  323.6 4.8 fusion.11.refs_1_
  328.4 1.4 multiply_add_fusion.3
  329.8 1.5 multiply_reduce_fusion.4
  331.4 1.8 multiply_reduce_fusion.3
  333.5 5.7 all-reduce.6
  340.1 2.1 subtract_convert_fusion.1
  343.1 1.3 pad_maximum_fusion.1
  344.4 2.6 copy.42
  347.0 6.9 fusion.8
  354.0 1.0 fusion.7
  355.2 1.9 pad_maximum_fusion.source
  357.1 25.4 %tensor_share.1 = bf16[800,512]{1,0:T(8,128)(2,1)} custom-call(bf16[800,2048]{1,0:T(8,128)(2,1)} %pad_maximum_fusion.source), custom_call_target="tpu_custom_call" | custom-call | tf_op jit(solution)/shard_map/tensor_share/pallas_call | solution.py:829
  382.5 2.4 fusion.14
  384.9 2.3 add_convert_fusion
  388.6 7.2 convert_bitcast_fusion.1.refs_0_
  395.8 299.4 %ring_sum.1 = (bf16[3,2048,512]{2,1,0:T(8,128)(2,1)}, bf16[1,512,2048]{2,1,0:T(8,128)(2,1)}, bf16[2,2048,512]{2,1,0:T(8,128)(2,1)}, bf16[2,256,2048]{2,1,0:T(8,128)(2,1)}, bf16[1,192,256]{2,1,0:T(8,128)(2,1)}) custom-call(bf16[3,2048,512]{2,1,0:T(8,128)(2,1)} %convert_bitcast_fusion.1.refs_0_, bf16[1,512,2048]{2,1,0:T(8,128)(2,1)} %fusion.11.refs_1_, ...), custom_call_target="tpu_custom_call" | custom-call | tf_op jit(solution)/shard_map/ring_sum/pallas_call | solution.py:141
  695.2 0.8 slice.125
  696.6 0.8 slice.127
  697.5 0.9 convert_element_type.152
  700.5 4.1 bitcast_convert_fusion
  704.6 2.5 convert_element_type.155
  707.1 9.5 %convert_bitcast_fusion = f32[2048,3,512]{2,0,1:T(8,128)} fusion(bf16[3,2048,512]{2,1,0:T(8,128)(2,1)} %get-tuple-element.64), kind=kLoop, calls=%fused_computation | loop fusion | flops 3145728 | bytes 18874368 | tf_op jit(solution)/shard_map/transpose | solution.py:1264
  716.6 9.6 %reshape.541 = f32[2,2048,2,256]{3,2,1,0:T(2,128)} reshape(bf16[2,2048,512]{2,1,0:T(8,128)(2,1)} %get-tuple-element.66) | data formatting | bytes 12582912 | tf_op jit(solution)/shard_map/reshape | solution.py:1266
  (118 shorter events, 19.4 us)
Async XLA Ops:
  0.6 141.3 %copy-start = (bf16[512,2048]{1,0:T(8,128)(2,1)S(1)}, bf16[512,2048]{1,0:T(8,128)(2,1)}, u32[]{:S(2)}) copy-start(bf16[512,2048]{1,0:T(8,128)(2,1)} %param.22) | copy-start | bytes 6291460
  10.6 8.8 %copy-start.32 = (f32[2048]{0:T(1024)S(1)}, f32[2048]{0:T(1024)}, u32[]{:S(2)}) copy-start(f32[2048]{0:T(1024)} %param.19) | copy-start | bytes 24580
  25.9 1.7 copy-start.14
  52.5 1.6 copy-start.8
  95.3 1.3 copy-start.2
  96.6 2.0 copy-start.4
  98.6 1.0 copy-start.5
  99.6 1.1 copy-start.6
  100.6 0.8 copy-start.7
  145.6 35.2 %copy-start.30 = (f32[2048]{0:T(1024)S(1)}, f32[2048]{0:T(1024)}, u32[]{:S(2)}) copy-start(f32[2048]{0:T(1024)} %param.23) | copy-start | bytes 24580
  177.6 3.2 copy-start.9
  177.6 3.5 copy-start.12
  180.7 2.8 copy-start.21
  182.2 1.3 copy-start.18
  228.4 2.5 copy-start.22
  228.4 2.5 copy-start.31
  228.7 2.2 copy-start.10
  228.7 2.6 copy-start.13
  231.4 1.9 copy-start.3
  236.4 2.0 copy-start.19
  256.1 67.5 %copy-start.27 = (bf16[512,512]{1,0:T(8,128)(2,1)S(1)}, bf16[512,512]{1,0:T(8,128)(2,1)}, u32[]{:S(2)}) copy-start(bf16[512,512]{1,0:T(8,128)(2,1)} %join_heads.1) | copy-start | bytes 1572868
  328.4 1.4 copy-start.17
  329.8 1.6 copy-start.16
  329.8 3.4 copy-start.15
  340.0 3.1 copy-start.28
  342.1 0.8 copy-start.24
  342.2 1.0 copy-start.25
  342.2 4.9 copy-start.11
  342.2 4.8 copy-start.29
  354.0 1.2 copy-start.26
  355.2 27.3 %copy-start.20 = (bf16[2,128,512]{2,1,0:T(8,128)(2,1)S(1)}, bf16[2,128,512]{2,1,0:T(8,128)(2,1)}, u32[]{:S(2)}) copy-start(bf16[2,128,512]{2,1,0:T(8,128)(2,1)} %get-tuple-element.47) | copy-start | bytes 786436
  695.2 9.4 %copy-start.23 = (bf16[2,256,2048]{2,1,0:T(8,128)(2,1)S(1)}, bf16[2,256,2048]{2,1,0:T(8,128)(2,1)}, u32[]{:S(2)}) copy-start(bf16[2,256,2048]{2,1,0:T(8,128)(2,1)} %get-tuple-element.67) | copy-start | bytes 6291460
  707.1 19.1 %copy-start.1 = (bf16[512,2048]{1,0:T(8,128)(2,1)S(1)}, bf16[512,2048]{1,0:T(8,128)(2,1)}, u32[]{:S(2)}) copy-start(bf16[512,2048]{1,0:T(8,128)(2,1)} %param.22) | copy-start | bytes 6291460
